TPU v7x, 256 devices: a whole 4x4x8 slice. The times are simulated.
256 devices in a mesh: slab: 32 (over y, z_lo, core), rows: 8 (over z_hi, x).
Axes of the slice: x: 4, y: 4, z: 8 (z_hi: 2, z_lo: 4; z = z_hi * 4 + z_lo), core: 2. Of those that a mesh axis runs over, the one named last changes fastest.
Arguments:
- volume: bfloat16 [64, 1024, 512], P('rows', 'slab'), may hold values from -6 to 6
- x_frequency: int32 [256, 2, 8], replicated, may hold values from 0 to 4095
- y_frequency: int32 [256, 2, 64], replicated, may hold values from 0 to 4095
- measured: float32 [256, 16, 128], P(('slab', 'rows')), may hold values from -6 to 6
- weights: float32 [256, 16, 64], P(('slab', 'rows')), may hold values from 0.25 to 4
Outputs:
- updated: bfloat16 [64, 1024, 512], P('rows', 'slab')
- residual: float32 [256, 16, 128], P(('slab', 'rows'))
Inputs may be any that keep to these rules, and one draw needn't show every extreme that they name: `x_frequency`: indices on a frequency grid of 4096 points. `y_frequency`: indices on a frequency grid of 4096 points.
All inputs are finite; a program needn't handle non-finite values.
Results may differ from a plain program's by a relative error of at most 0.0095.
Values may be sent and summed in bfloat16 or wider, within the bound.
No kernel may reach another device: no remote copies, remote signals or barrier semaphores. Data moves between devices by JAX's collectives and lax.ppermute only.
A program may use at most 64 MiB of HBM per device.

v0:
```python
import functools
import math

import jax
import jax.numpy as jnp
import numpy as np
from jax import lax
from jax.experimental import pallas as pl
from jax.experimental.pallas import tpu as pltpu
from jax.sharding import Mesh
from jax.sharding import PartitionSpec as P

FINE = 4096
GRAIN = 32
VMEM_LIMIT = 12 * 2**20
F32 = jnp.float32
BF16 = jnp.bfloat16
PEERS = ("y", "zl", "zh", "x")
SLAB = ("y", "zl", "c")
ROWS = ("zh", "x")


def column_table(length, scale, order):
    depths = np.arange(length, dtype=np.int64)
    angles = (order[:, None] * depths[None, :] % length) * (2.0 * math.pi / length)
    matrix = np.stack([np.cos(angles), -np.sin(angles)], axis=1) * scale
    return matrix.reshape(2 * len(order), length).astype(np.float32).astype(BF16)


def cosine_of_turns(turns):
    part = turns - jnp.floor(turns + 0.5)
    angle = (0.25 - jnp.abs(part)) * (2.0 * math.pi)
    square = angle * angle
    series = -1.0 / 39916800.0
    for term in (362880.0, -5040.0, 120.0, -6.0):
        series = series * square + 1.0 / term
    return angle + angle * square * series


def dot(left, right, left_dim, right_dim):
    dims = (((left_dim,), (right_dim,)), ((), ()))
    return lax.dot_general(left, right, dims, preferred_element_type=F32)


def low_half(shape, axis):
    return lax.broadcasted_iota(jnp.int32, shape, axis) < shape[axis] // 2


def exchange_grains(blocks):
    lane = lax.broadcasted_iota(jnp.int32, blocks[0].shape, blocks[0].ndim - 1)
    axis = blocks[0].ndim - 1
    low = lane < 2 * GRAIN
    even = (lane // GRAIN) % 2 == 0
    first = [None] * 4
    for i in (0, 1):
        a, b = blocks[i], blocks[i + 2]
        first[i] = jnp.where(low, a, pltpu.roll(b, 2 * GRAIN, axis))
        first[i + 2] = jnp.where(low, pltpu.roll(a, 2 * GRAIN, axis), b)
    last = [None] * 4
    for i in (0, 2):
        a, b = first[i], first[i + 1]
        last[i] = jnp.where(even, a, pltpu.roll(b, GRAIN, axis))
        last[i + 1] = jnp.where(even, pltpu.roll(a, 3 * GRAIN, axis), b)
    return last


def transform_kernel(columns_ref, table_ref, out_ref):
    spectrum = dot(table_ref[...], columns_ref[...], 1, 1)
    pairs = spectrum.shape[0] // 8
    near = spectrum[:, :128].reshape(pairs, 8, 128)
    far = spectrum[:, 128:].reshape(pairs, 8, 128)
    low = low_half(near.shape, 1)
    even = jnp.where(low, near, pltpu.roll(far, 4, 1))
    odd = jnp.where(low, pltpu.roll(near, 4, 1), far)
    out_ref[...] = jnp.concatenate([even, odd], axis=1).reshape(out_ref.shape).astype(BF16)


def predict_kernel(scale, planes_ref, y_ref, x_ref, out_ref):
    planes = planes_ref[...].astype(F32).reshape(4, 4, 64, 128)
    blocks = exchange_grains([planes[:, i] for i in range(4)])
    left = jnp.concatenate(
        [jnp.concatenate([b[i] for b in blocks], axis=0) for i in range(4)], axis=1
    ).astype(BF16)
    inner = dot(left, y_ref[...], 1, 0).astype(BF16)
    first = low_half((8, 128), 1)
    for p in range(2):
        parts = jnp.concatenate(
            [inner[:, 256 * p : 256 * p + 128], inner[:, 256 * p + 128 : 256 * p + 256]], axis=0
        )
        points = dot(x_ref[p], parts, 1, 0) * scale
        real, imag = points[:16], points[16:]
        out_ref[p, :8] = jnp.where(first, real[:8], pltpu.roll(imag[:8], 64, 1))
        out_ref[p, 8:] = jnp.where(first, pltpu.roll(real[8:], 64, 1), imag[8:])


def spread_kernel(scale, mine_ref, other_ref, target_ref, y_ref, x_ref, misfit_ref, out_ref):
    first = low_half((8, 128), 1)
    zero = jnp.zeros((8, 128), F32)
    pieces = []
    for p in range(2):
        points = mine_ref[p] + other_ref[p]
        misfit = target_ref[p, 16:] * (points - target_ref[p, :16])
        misfit_ref[p] = misfit
        near, far = misfit[:8], misfit[8:]
        spread = jnp.concatenate(
            [
                jnp.where(first, near, zero),
                jnp.where(first, zero, pltpu.roll(far, 64, 1)),
                jnp.where(first, pltpu.roll(near, 64, 1), zero),
                jnp.where(first, zero, far),
            ],
            axis=0,
        ).astype(BF16)
        inner = dot(x_ref[p], spread, 0, 0)
        pieces += [inner[:256], inner[256:]]
    inner = jnp.concatenate(pieces, axis=1).astype(BF16)
    planes = dot(inner, y_ref[...], 1, 1) * scale
    planes = planes.reshape(4, 64, 512)
    for i in range(4):
        blocks = exchange_grains([planes[q, :, 128 * i : 128 * i + 128] for q in range(4)])
        for g in range(4):
            out_ref[pl.ds((4 * i + g) * 64, 64), :] = blocks[g].astype(BF16)


def update_kernel(planes_ref, columns_ref, table_ref, out_ref):
    planes = planes_ref[...].astype(F32)
    planes = planes.reshape(planes.shape[0] // 16, 16, 128)
    even, odd = planes[:, :8], planes[:, 8:]
    low = low_half(even.shape, 1)
    near = jnp.where(low, even, pltpu.roll(odd, 4, 1)).reshape(-1, 128)
    far = jnp.where(low, pltpu.roll(even, 4, 1), odd).reshape(-1, 128)
    back = jnp.concatenate([near, far], axis=1).astype(BF16)
    correction = dot(back, table_ref[...], 0, 0)
    out_ref[...] = (columns_ref[...].astype(F32) - 0.5 * correction).astype(BF16)


def local_call(kernel, outs, flops, *operands):
    whole = pl.BlockSpec(memory_space=pltpu.VMEM)
    moved = sum(math.prod(a.shape) * a.dtype.itemsize for a in operands)
    return pl.pallas_call(
        kernel,
        out_shape=outs,
        in_specs=[whole] * len(operands),
        out_specs=jax.tree.map(lambda _: whole, outs),
        compiler_params=pltpu.CompilerParams(vmem_limit_bytes=VMEM_LIMIT),
        cost_estimate=pl.CostEstimate(flops=flops, bytes_accessed=moved, transcendentals=0),
    )(*operands)


def shards(volume, x_frequency, y_frequency, measured, weights):
    x_local, y_local, length = volume.shape
    cells = x_local * y_local
    planes = length // 2
    size = {a: lax.axis_size(a) for a in SLAB + ROWS}
    at = {a: lax.axis_index(a) for a in SLAB + ROWS}
    stacks = size["y"] * size["zl"]
    cores = size["c"]
    rows = size["zh"] * size["x"]
    x_total, y_total = x_local * rows, y_local * stacks * cores
    angles, kx_count, ky_count = x_frequency.shape[1], x_frequency.shape[2], y_frequency.shape[2]
    forward_scale = 1.0 / math.sqrt(x_total * y_total)
    back_scale = 1.0 / math.sqrt(angles * kx_count * ky_count)
    columns = volume.reshape(cells, length)
    order = np.arange(planes).reshape(stacks, cores, rows).transpose(0, 2, 1).reshape(-1)
    forward = column_table(length, 1.0 / math.sqrt(length), order)
    inverse = column_table(length, 1.0 / math.sqrt(planes), order)

    def exchange(array):
        peers = stacks * rows
        blocks = array.reshape(peers, array.shape[0] // peers, array.shape[1])
        blocks = lax.all_to_all(blocks, PEERS, split_axis=0, concat_axis=0, tiled=True)
        return blocks.reshape(array.shape)

    swap = [(0, 1), (1, 0)]
    sending = local_call(
        transform_kernel,
        jax.ShapeDtypeStruct((4 * cells, 128), BF16),
        2 * cells * length * length,
        columns,
        forward,
    )

    start = (at["y"] * size["zl"] + at["zl"]) * cores * rows + at["zh"] * size["x"] + at["x"]
    half = FINE // 2

    def of_chip(array):
        taken = lax.dynamic_slice_in_dim(array, start, (cores - 1) * rows + 1, 0)[::rows]
        return (taken + half).astype(F32)

    ky = of_chip(y_frequency).reshape(cores, 1, angles * ky_count)
    ky = jnp.broadcast_to(ky, (cores, 2, angles * ky_count)).reshape(1, -1)
    part = np.tile(np.repeat(np.arange(2), angles * ky_count), cores).reshape(1, -1)
    steps = np.arange(stacks * y_local)
    steps = steps // y_local * (cores * y_local) + steps % y_local
    y_at = jnp.asarray(steps, F32).reshape(-1, 1) + (at["c"] * y_local).astype(F32)
    y_table = cosine_of_turns((ky * y_at + part * (FINE // 4)) * (1.0 / FINE)).astype(BF16)

    kx = of_chip(x_frequency).reshape(cores, 1, angles * kx_count, 1)
    kx = jnp.broadcast_to(kx, (cores, 2, angles * kx_count, 1)).reshape(cores, -1, 1)
    point_part = np.repeat(np.arange(2), angles * kx_count).reshape(1, -1, 1)
    halves = cells // 128
    inside = x_local // halves
    grid = np.indices((2, inside, rows, halves, cores, 2)).reshape(6, 1, 1, -1)
    x_at = grid[2] * x_local + grid[3] * inside + grid[1]
    quarter = 3 * (grid[0] + grid[5]) + point_part
    same = grid[4] == np.arange(cores).reshape(-1, 1, 1)
    x_table = cosine_of_turns((kx * x_at + quarter * (FINE // 4)) * (1.0 / FINE))
    x_table = jnp.where(same, x_table, 0.0).astype(BF16)

    mine = jnp.concatenate([measured[0], jnp.concatenate([weights[0], weights[0]], -1)], 0)
    mine, sending = lax.optimization_barrier((mine, sending))
    other = lax.ppermute(mine, "c", swap)
    received = exchange(sending)
    target = jnp.where(at["c"] == 0, jnp.stack([mine, other]), jnp.stack([other, mine]))

    points = local_call(
        functools.partial(predict_kernel, forward_scale),
        jax.ShapeDtypeStruct((cores,) + measured.shape[1:], F32),
        2 * cells * length * length,
        received,
        y_table,
        x_table,
    )
    others = lax.ppermute(points, "c", swap)
    misfit, sending = local_call(
        functools.partial(spread_kernel, back_scale),
        (jax.ShapeDtypeStruct(points.shape, F32), jax.ShapeDtypeStruct(received.shape, BF16)),
        2 * cells * length * length,
        points,
        others,
        target,
        y_table,
        x_table,
    )
    received = exchange(sending)
    residual = lax.dynamic_slice_in_dim(misfit, at["c"], 1, 0)
    updated = local_call(
        update_kernel,
        jax.ShapeDtypeStruct(columns.shape, BF16),
        2 * cells * length * length,
        received,
        columns,
        inverse,
    )
    return (updated.reshape(volume.shape), residual)


def solution(mesh):
    fine = Mesh(mesh.devices.reshape(4, 4, 2, 2, 4), ("y", "zl", "c", "zh", "x"))
    placed = (
        P(ROWS, SLAB, None),
        P(),
        P(),
        P(SLAB + ROWS, None, None),
        P(SLAB + ROWS, None, None),
    )
    return jax.shard_map(
        shards,
        mesh=fine,
        in_specs=placed,
        out_specs=(P(ROWS, SLAB, None), P(SLAB + ROWS, None, None)),
        check_vma=False,
    )
```

profile of v0, /device:TPU:32, one launch (start us, length us, event | category | flops | bytes accessed | tf_op | source)
XLA Modules:
  0.0 59.2 jit_solution(10426567646149585579)
XLA Ops:
  0.6 0.0 copy-start
  0.6 0.8 %maximum_maximum_fusion = f32[32,128]{1,0:T(8,128)S(1)} fusion(f32[16,64]{1,0:T(8,128)} %bitcast.23, f32[16,128]{1,0:T(8,128)} %bitcast.24), kind=kLoop, calls=%fused_computation.27 | loop fusion | flops 8192 | bytes 28672 | tf_op jit(solution)/shard_map/concatenate | solution.py:210
  1.5 0.0 copy-start.1
  1.5 0.9 %copy-done.1 = bf16[8,32,512]{2,1,0:T(8,128)(2,1)S(1)} copy-done((bf16[8,32,512]{2,1,0:T(8,128)(2,1)S(1)}, bf16[8,32,512]{2,1,0:T(8,128)(2,1)}, u32[]{:S(2)}) %copy-start.1) | copy-done | bytes 262168
  2.4 0.0 copy-start.4
  2.4 1.0 %copy-done.4 = bf16[512,512]{1,0:T(8,128)(2,1)S(1)} copy-done((bf16[512,512]{1,0:T(8,128)(2,1)S(1)}, bf16[512,512]{1,0:T(8,128)(2,1)}, u32[]{:S(2)}) %copy-start.4) | copy-done | bytes 524312
  3.5 1.0 %shard_map.131 = bf16[1024,128]{1,0:T(8,128)(2,1)} custom-call(bf16[256,512]{1,0:T(8,128)(2,1)S(1)} %bitcast.15, bf16[512,512]{1,0:T(8,128)(2,1)S(1)} %copy-done.4), custom_call_target="tpu_custom_call" | custom-call | flops 134217728 | bytes 786432 | tf_op jit(solution)/shard_map/pallas_call | solution.py:140
  4.5 15.0 %all-to-all-start = ((bf16[128,8,128]{2,1,0:T(8,128)(2,1)}), bf16[128,8,128]{2,1,0:T(8,128)(2,1)S(1)}, u32[]{:S(2)}, u32[]{:S(2)}) async-start(bf16[128,8,128]{2,1,0:T(8,128)(2,1)} %bitcast.3), calls=%async_computation | async-start | bytes 524288 | tf_op jit(solution)/shard_map/all_to_all | solution.py:171
  19.5 0.1 collective-permute-start.1
  19.6 0.0 copy-start.6
  19.7 0.7 %copy-done.6 = s32[256,2,8]{0,2,1:T(8,128)S(1)} copy-done((s32[256,2,8]{0,2,1:T(8,128)S(1)}, s32[256,2,8]{0,2,1:T(8,128)}, u32[]{:S(2)}) %copy-start.6) | copy-done | bytes 16408
  20.4 0.1 constant_dynamic-slice_fusion.1
  20.4 0.1 slice.7
  20.5 0.0 copy-done
  20.5 0.1 constant_dynamic-slice_fusion.2
  20.6 0.1 slice.6
  20.7 0.0 copy-start.10
  20.7 0.7 %copy-done.10 = f32[512]{0:T(512)S(1)} copy-done((f32[512]{0:T(512)S(1)}, f32[512]{0:T(512)}, u32[]{:S(2)}) %copy-start.10) | copy-done | bytes 2072
  21.4 0.1 copy.16
  21.5 0.1 broadcast_in_dim.36
  21.6 0.1 copy.14
  21.6 0.0 copy-start.9
  21.6 0.7 %copy-done.9 = f32[512]{0:T(512)S(1)} copy-done((f32[512]{0:T(512)S(1)}, f32[512]{0:T(512)}, u32[]{:S(2)}) %copy-start.9) | copy-done | bytes 2072
  22.3 0.0 copy-start.5
  22.3 0.0 copy-start.7
  22.3 0.0 copy-start.8
  22.3 0.8 %fusion.2.y_ref = bf16[512,512]{1,0:T(8,128)(2,1)S(1)} fusion(f32[512]{0:T(512)S(1)} %copy-done.9, f32[512]{0:T(512)S(1)} %broadcast_add_fusion, f32[512]{0:T(512)S(1)} %bitcast.22), kind=kLoop, calls=%fused_computation.7 | loop fusion | flops 5767168 | bytes 530432 | tf_op jit(solution)/shard_map/convert_element_type | solution.py:196
  23.2 0.0 copy-done.5
  23.2 0.0 copy-done.7
  23.2 0.0 copy-done.8
  23.2 0.2 fusion.10.x_ref
  23.4 10.4 %all-to-all-done = bf16[128,8,128]{2,1,0:T(8,128)(2,1)S(1)} async-done(((bf16[128,8,128]{2,1,0:T(8,128)(2,1)}), bf16[128,8,128]{2,1,0:T(8,128)(2,1)S(1)}, u32[]{:S(2)}, u32[]{:S(2)}) %all-to-all-start) | async-done | bytes 262176 | tf_op jit(solution)/shard_map/all_to_all | solution.py:171
  33.8 0.7 %shard_map.132.mine_ref = f32[2,16,128]{2,1,0:T(8,128)S(1)} custom-call(bf16[1024,128]{1,0:T(8,128)(2,1)S(1)} %bitcast.17, bf16[512,512]{1,0:T(8,128)(2,1)S(1)} %fusion.2.y_ref, bf16[2,32,512]{2,1,0:T(8,128)(2,1)S(1)} %fusion.10.x_ref), custom_call_target="tpu_custom_call" | custom-call | flops 134217728 | bytes 851968 | tf_op jit(solution)/shard_map/pallas_call | solution.py:140
  34.5 0.1 collective-permute-start
  34.5 0.0 collective-permute-done.1
  34.6 0.0 copy-start.3
  34.6 1.1 %collective-permute-done.other_ref = f32[2,16,128]{2,1,0:T(8,128)S(1)} collective-permute-done((f32[2,16,128]{2,1,0:T(8,128)S(1)}, f32[2,16,128]{2,1,0:T(8,128)S(1)}, u32[]{:S(2)}, u32[]{:S(2)}) %collective-permute-start) | collective-permute-done | bytes 16416 | tf_op jit(solution)/shard_map/ppermute | solution.py:224
  35.7 1.4 %shard_map.133 = (f32[2,16,128]{2,1,0:T(8,128)S(1)}, bf16[1024,128]{1,0:T(8,128)(2,1)}) custom-call(f32[2,16,128]{2,1,0:T(8,128)S(1)} %shard_map.132.mine_ref, f32[2,16,128]{2,1,0:T(8,128)S(1)} %collective-permute-done.other_ref, f32[2,32,128]{2,1,0:T(8,128)S(1)} %maximum_select_fusion.target_ref, bf16[512,512]{1,0:T(8,128)(2,1)S(1)} %fusion.2.y_ref, ...), custom_call_target="tpu_custom_call" | custom-call | flops 134217728 | bytes 655360 | tf_op jit(solution)/shard_map/pallas_call | solution.py:140
  37.1 0.0 copy-start.2
  37.1 6.6 %all-to-all-start.1 = ((bf16[128,8,128]{2,1,0:T(8,128)(2,1)}), bf16[128,8,128]{2,1,0:T(8,128)(2,1)S(1)}, u32[]{:S(2)}, u32[]{:S(2)}) async-start(bf16[128,8,128]{2,1,0:T(8,128)(2,1)} %bitcast.10), calls=%async_computation.1 | async-start | bytes 524288 | tf_op jit(solution)/shard_map/all_to_all | solution.py:171
  43.7 0.6 %constant_dynamic-slice_fusion = f32[1,16,128]{2,1,0:T(8,128)} fusion(f32[2,16,128]{2,1,0:T(8,128)S(1)} %get-tuple-element.9, s32[]{:T(128)S(6)} %select_n.23), kind=kLoop, calls=%fused_computation.30 | loop fusion | bytes 16388 | tf_op jit(solution)/shard_map/dynamic_slice | solution.py:236
  44.3 13.9 %all-to-all-done.1 = bf16[128,8,128]{2,1,0:T(8,128)(2,1)S(1)} async-done(((bf16[128,8,128]{2,1,0:T(8,128)(2,1)}), bf16[128,8,128]{2,1,0:T(8,128)(2,1)S(1)}, u32[]{:S(2)}, u32[]{:S(2)}) %all-to-all-start.1) | async-done | bytes 262176 | tf_op jit(solution)/shard_map/all_to_all | solution.py:171
  58.2 0.0 copy-done.3
  58.2 0.0 copy-done.2
  58.2 1.0 %shard_map.134 = bf16[256,512]{1,0:T(8,128)(2,1)} custom-call(bf16[1024,128]{1,0:T(8,128)(2,1)S(1)} %bitcast.14, bf16[256,512]{1,0:T(8,128)(2,1)S(1)} %bitcast.16, bf16[512,512]{1,0:T(8,128)(2,1)S(1)} %copy-done.3), custom_call_target="tpu_custom_call" | custom-call | flops 134217728 | bytes 1048576 | tf_op jit(solution)/shard_map/pallas_call | solution.py:140
  (6 shorter events, 0.0 us)
Async XLA Ops:
  0.6 19.9 %copy-start = (s32[256,2,64]{0,2,1:T(8,128)S(1)}, s32[256,2,64]{0,2,1:T(8,128)}, u32[]{:S(2)}) copy-start(s32[256,2,64]{0,2,1:T(8,128)} %param.14) | copy-start | bytes 393220
  1.5 1.0 %copy-start.1 = (bf16[8,32,512]{2,1,0:T(8,128)(2,1)S(1)}, bf16[8,32,512]{2,1,0:T(8,128)(2,1)}, u32[]{:S(2)}) copy-start(bf16[8,32,512]{2,1,0:T(8,128)(2,1)} %param.12) | copy-start | bytes 786436
  2.4 1.0 %copy-start.4 = (bf16[512,512]{1,0:T(8,128)(2,1)S(1)}, bf16[512,512]{1,0:T(8,128)(2,1)}, u32[]{:S(2)}) copy-start(bf16[512,512]{1,0:T(8,128)(2,1)} %constant.28.clone.table_ref) | copy-start | bytes 1572868
  4.5 29.2 %all-to-all-start = ((bf16[128,8,128]{2,1,0:T(8,128)(2,1)}), bf16[128,8,128]{2,1,0:T(8,128)(2,1)S(1)}, u32[]{:S(2)}, u32[]{:S(2)}) async-start(bf16[128,8,128]{2,1,0:T(8,128)(2,1)} %bitcast.3), calls=%async_computation | async-start | bytes 524288 | tf_op jit(solution)/shard_map/all_to_all | solution.py:171
  19.5 15.0 %collective-permute-start.1 = (f32[32,128]{1,0:T(8,128)S(1)}, f32[32,128]{1,0:T(8,128)S(1)}, u32[]{:S(2)}, u32[]{:S(2)}) collective-permute-start(f32[32,128]{1,0:T(8,128)S(1)} %maximum_maximum_fusion), channel_id=1, source_target_pairs={{0,8},{8,0},{1,9},{9,1},{2,10},{10,2},{3,11},{11,3},{4,12},{12,4},... | collective-permute-start | bytes 49160 | tf_op jit(solution)/shard_map/ppermute | solution.py:212
  19.6 0.7 %copy-start.6 = (s32[256,2,8]{0,2,1:T(8,128)S(1)}, s32[256,2,8]{0,2,1:T(8,128)}, u32[]{:S(2)}) copy-start(s32[256,2,8]{0,2,1:T(8,128)} %param.13) | copy-start | bytes 49156
  20.7 0.7 %copy-start.10 = (f32[512]{0:T(512)S(1)}, f32[512]{0:T(512)}, u32[]{:S(2)}) copy-start(f32[512]{0:T(512)} %constant.80.clone) | copy-start | bytes 6148
  21.6 0.7 %copy-start.9 = (f32[512]{0:T(512)S(1)}, f32[512]{0:T(512)}, u32[]{:S(2)}) copy-start(f32[512]{0:T(512)} %constant.89) | copy-start | bytes 6148
  22.3 0.8 %copy-start.5 = (f32[32,512]{1,0:T(8,128)S(1)}, f32[32,512]{1,0:T(8,128)}, u32[]{:S(2)}) copy-start(f32[32,512]{1,0:T(8,128)} %constant.94) | copy-start | bytes 196612
  22.3 0.8 %copy-start.7 = (f32[512]{0:T(512)S(1)}, f32[512]{0:T(512)}, u32[]{:S(2)}) copy-start(f32[512]{0:T(512)} %constant.92) | copy-start | bytes 6148
  22.3 0.8 %copy-start.8 = (pred[2,512]{1,0:T(4,128)(4,1)S(1)}, pred[2,512]{1,0:T(4,128)(4,1)}, u32[]{:S(2)}) copy-start(pred[2,512]{1,0:T(4,128)(4,1)} %constant.90) | copy-start | bytes 3076
  34.5 1.2 %collective-permute-start = (f32[2,16,128]{2,1,0:T(8,128)S(1)}, f32[2,16,128]{2,1,0:T(8,128)S(1)}, u32[]{:S(2)}, u32[]{:S(2)}) collective-permute-start(f32[2,16,128]{2,1,0:T(8,128)S(1)} %shard_map.132.mine_ref), channel_id=1, source_target_pairs={{0,8},{8,0},{1,9},{9,1},{2,10},{10,2},{3,11},{11,3},{4,12},{12,4},... | collective-permute-start | bytes 49160 | tf_op jit(solution)/shard_map/ppermute | solution.py:224
  34.6 23.6 %copy-start.3 = (bf16[512,512]{1,0:T(8,128)(2,1)S(1)}, bf16[512,512]{1,0:T(8,128)(2,1)}, u32[]{:S(2)}) copy-start(bf16[512,512]{1,0:T(8,128)(2,1)} %constant.85.clone.table_ref) | copy-start | bytes 1572868
  37.1 21.1 %copy-start.2 = (bf16[8,32,512]{2,1,0:T(8,128)(2,1)S(1)}, bf16[8,32,512]{2,1,0:T(8,128)(2,1)}, u32[]{:S(2)}) copy-start(bf16[8,32,512]{2,1,0:T(8,128)(2,1)} %param.12) | copy-start | bytes 786436
  37.1 21.1 %all-to-all-start.1 = ((bf16[128,8,128]{2,1,0:T(8,128)(2,1)}), bf16[128,8,128]{2,1,0:T(8,128)(2,1)S(1)}, u32[]{:S(2)}, u32[]{:S(2)}) async-start(bf16[128,8,128]{2,1,0:T(8,128)(2,1)} %bitcast.10), calls=%async_computation.1 | async-start | bytes 524288 | tf_op jit(solution)/shard_map/all_to_all | solution.py:171
where the time goes:
time: 59.7 us; the launch traced here: 59.2 us
  waiting for transfers between devices  25.5 us (43%)
  starting transfers between devices  21.7 us (36%)
  local copies, waits for them, and re-layouts  5.29 us (9%)
  Pallas kernels  4.17 us (7%)
  other arithmetic  1.85 us (3%)
  between operations  0.77 us (1%)
    all_to_all x2, waiting for transfers between devices, exchange(): lax.all_to_all(blocks, PEERS, split_axis=0, concat_axis=0, tiled=True)  24.3 us
    all_to_all x2, starting transfers between devices, exchange(): lax.all_to_all(blocks, PEERS, split_axis=0, concat_axis=0, tiled=True)  21.6 us
    pallas_call x4, Pallas kernels, local_call(): pl.pallas_call(kernel, out_shape=outs, in_specs=[whole] * len(operands),...  4.17 us
    unnamed x22, local copies, waits for them, and re-layouts  4.12 us
  transfers between devices with their start and end apart: 4, of which 3 were waited for; matrix products, arithmetic and copies ran while one was open for 4% of the time, Pallas kernels for 1%

commit v1 on v0

v1 whole, which is shorter than its diff:
```python
import functools
import math

import jax
import jax.numpy as jnp
import numpy as np
from jax import lax
from jax.experimental import pallas as pl
from jax.experimental.pallas import tpu as pltpu
from jax.sharding import Mesh
from jax.sharding import PartitionSpec as P

FINE = 4096
GRAIN = 32
LANES = 128
CHUNKS = 4
VMEM_LIMIT = 12 * 2**20
VMEM_ALL = 61 * 2**20
F32 = jnp.float32
BF16 = jnp.bfloat16
AXES = {"yh": 2, "yl": 2, "zl": 4, "c": 2, "zh": 2, "xh": 2, "xl": 2}
SLAB = ("yh", "yl", "zl", "c")
ROWS = ("zh", "xh", "xl")
PEERS = ("yl", "zl", "zh", "xl")
TEAM = ("yh", "c", "xh")
PLANES = 8
SWAP = [(0, 1), (1, 0)]


def plane_of(**at):
    number = 0
    for axis in SLAB + ROWS:
        number = number * AXES[axis] + at[axis]
    return number


def column_table(length, scale):
    grid = np.arange(length // 2).reshape([AXES[a] for a in SLAB + ROWS])
    order = grid.transpose([(SLAB + ROWS).index(a) for a in PEERS + TEAM]).reshape(-1)
    depths = np.arange(length, dtype=np.int64)
    angles = (order[:, None] * depths[None, :] % length) * (2.0 * math.pi / length)
    matrix = np.stack([np.cos(angles), -np.sin(angles)], axis=1) * scale
    return matrix.reshape(length, length).astype(np.float32).astype(BF16)


def cosine_of_turns(turns):
    part = turns - jnp.floor(turns + 0.5)
    angle = (0.25 - jnp.abs(part)) * (2.0 * math.pi)
    square = angle * angle
    series = -1.0 / 39916800.0
    for term in (362880.0, -5040.0, 120.0, -6.0):
        series = series * square + 1.0 / term
    return angle + angle * square * series


def dot(left, right, left_dim, right_dim):
    dims = (((left_dim,), (right_dim,)), ((), ()))
    return lax.dot_general(left, right, dims, preferred_element_type=F32)


def iota(shape, axis):
    return lax.broadcasted_iota(jnp.int32, shape, axis)


def exchange_grains(blocks):
    lane = iota(blocks[0].shape, 1)
    low = lane < 2 * GRAIN
    even = (lane & GRAIN) == 0
    first = [None] * 4
    for i in (0, 1):
        a, b = blocks[i], blocks[i + 2]
        first[i] = jnp.where(low, a, pltpu.roll(b, 2 * GRAIN, 1))
        first[i + 2] = jnp.where(low, pltpu.roll(a, 2 * GRAIN, 1), b)
    last = [None] * 4
    for i in (0, 2):
        a, b = first[i], first[i + 1]
        last[i] = jnp.where(even, a, pltpu.roll(b, GRAIN, 1))
        last[i + 1] = jnp.where(even, pltpu.roll(a, 3 * GRAIN, 1), b)
    return last


def transform_kernel(columns_hbm, table_hbm, out_hbm, columns, table, staged, sems, out_sems):
    rows = table.shape[0] // CHUNKS
    first = pltpu.make_async_copy(columns_hbm, columns, sems.at[CHUNKS])
    first.start()
    loads = []
    for i in range(CHUNKS):
        part = pl.ds(i * rows, rows)
        loads.append(pltpu.make_async_copy(table_hbm.at[part], table.at[part], sems.at[i]))
        loads[-1].start()
    first.wait()
    stores = []
    for i in range(CHUNKS):
        loads[i].wait()
        spectrum = dot(table[pl.ds(i * rows, rows), :], columns[...], 1, 1).astype(BF16)
        near = spectrum[:, :LANES].reshape(rows // 16, 16, LANES)
        far = spectrum[:, LANES:].reshape(rows // 16, 16, LANES)
        part = pl.ds(i * 2 * rows, 2 * rows)
        staged[part, :] = jnp.stack([near, far], axis=1).reshape(2 * rows, LANES)
        stores.append(pltpu.make_async_copy(staged.at[part], out_hbm.at[part], out_sems.at[i]))
        stores[-1].start()
    for store in stores:
        store.wait()


def tables_kernel(x_ref, y_ref, x_table_ref, y_table_ref, turned):
    at = {a: lax.axis_index(a) for a in SLAB + ROWS}
    turned[...] = y_ref[...].astype(F32).T
    x_all = x_ref[...].astype(F32)
    lane_plane = iota(x_all.shape, 1)
    lane = iota((32, LANES), 1)
    row = iota((32, LANES), 0)
    x_at = ((lane >> 2) & 1) * 32 + at["xh"] * 16 + ((lane >> 1) & 1) * 8
    x_at = (x_at + (lane & 1) * 4 + ((lane >> 3) & 3)).astype(F32)
    quarter = 3 * ((lane >> 6) + ((lane >> 5) & 1)) + (row >> 4)
    x_shift = (quarter * (FINE // 4)).astype(F32)
    y_in = iota((32, LANES), 0).astype(F32)
    block = iota((8, LANES), 0)
    y_block = at["yh"] * 512 + (block >> 2) * 256 + (block & 3) * 64 + at["c"] * 32
    y_block = y_block.astype(F32)
    for p in range(PLANES):
        plane = plane_of(**{**at, "yh": p >> 2, "c": (p >> 1) & 1, "xh": p & 1})
        kx = jnp.sum(jnp.where(lane_plane == plane, x_all, 0.0), axis=1, keepdims=True)
        kx = jnp.concatenate([kx, kx], axis=0) + FINE / 2.0
        x_table_ref[p] = cosine_of_turns((kx * x_at + x_shift) * (1.0 / FINE)).astype(BF16)
        ky = (turned[pl.ds(plane, 1), :] + FINE / 2.0) * (1.0 / FINE)
        fine = ky * y_in
        fine_real, fine_imag = cosine_of_turns(fine), cosine_of_turns(fine + 0.25)
        coarse = ky * y_block
        coarse_real, coarse_imag = cosine_of_turns(coarse), cosine_of_turns(coarse + 0.25)
        for b in range(8):
            real, imag = coarse_real[b : b + 1], coarse_imag[b : b + 1]
            rows = pl.ds(b * 32, 32)
            y_table_ref[p, rows, :LANES] = (real * fine_real - imag * fine_imag).astype(BF16)
            y_table_ref[p, rows, LANES:] = (real * fine_imag + imag * fine_real).astype(BF16)


def own_plane():
    return (lax.axis_index("yh") * 2 + lax.axis_index("c")) * 2 + lax.axis_index("xh")


def predict_kernel(
    scale, planes_ref, y_ref, x_ref, measured_ref, weights_ref, out_ref, sent_ref, turned
):
    planes = planes_ref[...].astype(F32).reshape(2, 4, LANES, LANES)
    for i in range(2):
        blocks = exchange_grains([planes[i, g] for g in range(4)])
        for q in range(4):
            turned[i, pl.ds(q * LANES, LANES), :] = blocks[q]
    first = iota((8, LANES), 1) < LANES // 2
    for p in range(PLANES):
        left = [
            jnp.concatenate(
                [turned[i, pl.ds(2 * p + part, 32, stride=16), :] for i in range(2)], axis=1
            )
            for part in range(2)
        ]
        left = jnp.concatenate(left, axis=0).astype(BF16)
        inner = dot(left, y_ref[p], 1, 0).astype(BF16)
        inner = jnp.concatenate([inner[:, :LANES], inner[:, LANES:]], axis=0)
        points = dot(x_ref[p], inner, 1, 0) * scale
        real, imag = points[:16], points[16:]
        out_ref[p, :8] = jnp.where(first, real[:8], pltpu.roll(imag[:8], 64, 1))
        out_ref[p, 8:16] = jnp.where(first, pltpu.roll(real[8:], 64, 1), imag[8:])
        out_ref[p, 16:] = jnp.zeros((8, LANES), F32)
    own = own_plane()
    out_ref[own, :16] = out_ref[own, :16] - measured_ref[...]
    out_ref[own, 16:] = weights_ref[...]
    sent_ref[...] = out_ref[...].astype(BF16)


def spread_kernel(
    scale, sum_ref, other_ref, y_ref, x_ref, misfit_ref, out_hbm, turned, staged, sems
):
    first = iota((8, LANES), 1) < LANES // 2

    def misfit_of(total):
        near, far, weight = total[:8], total[8:16], total[16:]
        crossed = pltpu.roll(weight, 64, 1)
        return (
            near * jnp.where(first, weight, crossed),
            far * jnp.where(first, crossed, weight),
        )

    zero = jnp.zeros((8, LANES), F32)
    for p in range(PLANES):
        near, far = misfit_of(sum_ref[p] + other_ref[p].astype(F32))
        spread = jnp.concatenate(
            [
                jnp.where(first, near, zero),
                jnp.where(first, zero, pltpu.roll(far, 64, 1)),
                jnp.where(first, pltpu.roll(near, 64, 1), zero),
                jnp.where(first, zero, far),
            ],
            axis=0,
        ).astype(BF16)
        inner = dot(x_ref[p], spread, 0, 0).astype(BF16)
        inner = jnp.concatenate([inner[:64], inner[64:]], axis=1)
        planes = dot(inner, y_ref[p], 1, 1) * scale
        for part in range(2):
            for i in range(2):
                turned[i, pl.ds(2 * p + part, 32, stride=16), :] = planes[
                    part * 32 : part * 32 + 32, i * LANES : i * LANES + LANES
                ]
    stores = []
    for i in range(2):
        blocks = exchange_grains([turned[i, pl.ds(q * LANES, LANES), :] for q in range(4)])
        for g in range(4):
            staged[pl.ds((4 * i + g) * LANES, LANES), :] = blocks[g].astype(BF16)
        part = pl.ds(i * 4 * LANES, 4 * LANES)
        stores.append(pltpu.make_async_copy(staged.at[part], out_hbm.at[part], sems.at[i]))
        stores[-1].start()
    own = own_plane()
    near, far = misfit_of(sum_ref[own] + other_ref[own].astype(F32))
    misfit_ref[:8], misfit_ref[8:] = near, far
    for store in stores:
        store.wait()


def update_kernel(planes_ref, columns_ref, table_ref, out_hbm, staged, sems):
    planes = planes_ref[...].reshape(planes_ref.shape[0] // 32, 2, 16, LANES)
    table = table_ref[...]
    stores = []
    for i in range(2):
        part = pl.ds(i * LANES, LANES)
        correction = dot(planes[:, i].reshape(-1, LANES), table, 0, 0)
        staged[part, :] = (columns_ref[part, :].astype(F32) - 0.5 * correction).astype(BF16)
        stores.append(pltpu.make_async_copy(staged.at[part], out_hbm.at[part], sems.at[i]))
        stores[-1].start()
    for store in stores:
        store.wait()


VMEM = pl.BlockSpec(memory_space=pltpu.VMEM)
HBM = pl.BlockSpec(memory_space=pltpu.HBM)


def local_call(kernel, outs, scratch, operands, specs=None, out_specs=None, limit=VMEM_LIMIT):
    moved = sum(math.prod(a.shape) * a.dtype.itemsize for a in operands)
    return pl.pallas_call(
        kernel,
        out_shape=outs,
        in_specs=specs or [VMEM] * len(operands),
        out_specs=jax.tree.map(lambda _: VMEM, outs) if out_specs is None else out_specs,
        scratch_shapes=scratch,
        compiler_params=pltpu.CompilerParams(vmem_limit_bytes=limit),
        cost_estimate=pl.CostEstimate(flops=2**27, bytes_accessed=moved, transcendentals=0),
    )(*operands)


def shape_of(*shape, dtype=BF16):
    return jax.ShapeDtypeStruct(shape, dtype)


def exchange(array):
    peers = math.prod(AXES[a] for a in PEERS)
    blocks = array.reshape(peers, array.shape[0] // peers, array.shape[1])
    blocks = lax.all_to_all(blocks, PEERS, split_axis=0, concat_axis=0, tiled=True)
    return blocks.reshape(array.shape)


def shards(volume, x_frequency, y_frequency, measured, weights):
    x_local, y_local, length = volume.shape
    cells = x_local * y_local
    rows = cells * length // LANES
    planes, angles, kx_count = x_frequency.shape
    ky_count = y_frequency.shape[2]
    cells_total = cells * math.prod(AXES.values())
    forward_scale = 1.0 / math.sqrt(cells_total)
    back_scale = 1.0 / math.sqrt(angles * kx_count * ky_count)
    columns = volume.reshape(cells, length)
    forward = column_table(length, 1.0 / math.sqrt(length))
    inverse = column_table(length, 1.0 / math.sqrt(planes))

    sending = local_call(
        transform_kernel,
        shape_of(rows, LANES),
        [
            pltpu.VMEM((cells, length), BF16),
            pltpu.VMEM((length, length), BF16),
            pltpu.VMEM((rows, LANES), BF16),
            pltpu.SemaphoreType.DMA((CHUNKS + 1,)),
            pltpu.SemaphoreType.DMA((CHUNKS,)),
        ],
        (columns, forward),
        [HBM, HBM],
        HBM,
        VMEM_ALL,
    )
    received = exchange(sending)

    x_table, y_table = local_call(
        tables_kernel,
        (shape_of(PLANES, 32, LANES), shape_of(PLANES, 256, 256)),
        [pltpu.VMEM((planes, LANES), F32)],
        (
            x_frequency.transpose(1, 2, 0).reshape(angles * kx_count, planes),
            y_frequency.transpose(1, 2, 0).reshape(angles * ky_count, planes),
        ),
    )
    packed = jnp.concatenate([weights[0, :kx_count], weights[0, kx_count:]], axis=-1)
    packed, sending = lax.optimization_barrier((packed, sending))

    work = shape_of(PLANES, 24, LANES, dtype=F32)
    turned = pltpu.VMEM((2, 4 * LANES, LANES), F32)
    total, sent = local_call(
        functools.partial(predict_kernel, forward_scale),
        (work, shape_of(PLANES, 24, LANES)),
        [turned],
        (received, y_table, x_table, measured[0], packed),
    )
    total = total + lax.ppermute(sent, "c", SWAP).astype(F32)
    total = total + lax.ppermute(total.astype(BF16), "xh", SWAP).astype(F32)
    other = lax.ppermute(total.astype(BF16), "yh", SWAP)
    misfit, sending = local_call(
        functools.partial(spread_kernel, back_scale),
        (shape_of(angles * kx_count, LANES, dtype=F32), shape_of(rows, LANES)),
        [turned, pltpu.VMEM((rows, LANES), BF16), pltpu.SemaphoreType.DMA((2,))],
        (total, other, y_table, x_table),
        None,
        (VMEM, HBM),
    )
    received = exchange(sending)
    updated = local_call(
        update_kernel,
        shape_of(cells, length),
        [pltpu.VMEM((cells, length), BF16), pltpu.SemaphoreType.DMA((2,))],
        (received, columns, inverse),
        None,
        HBM,
    )
    return (updated.reshape(volume.shape), misfit.reshape(measured.shape))


def solution(mesh):
    fine = Mesh(mesh.devices.reshape(tuple(AXES.values())), tuple(AXES))
    placed = (
        P(ROWS, SLAB, None),
        P(),
        P(),
        P(SLAB + ROWS, None, None),
        P(SLAB + ROWS, None, None),
    )
    return jax.shard_map(
        shards,
        mesh=fine,
        in_specs=placed,
        out_specs=(P(ROWS, SLAB, None), P(SLAB + ROWS, None, None)),
        check_vma=False,
    )
```

time: 59.7 us -> 60 us (level)
  the two profiles are of different devices: /device:TPU:32 before, /device:TPU:16 now
where the time goes in v1:
time: 60 us; the launch traced here: 59.7 us
  waiting for transfers between devices  20.5 us (34%)
  blocking collectives  14.7 us (24%)
  starting transfers between devices  14.3 us (24%)
  Pallas kernels  8.7 us (14%)
  between operations  0.74 us (1%)
  local copies, waits for them, and re-layouts  0.65 us (1%)
    all_to_all x1, blocking collectives, exchange(): lax.all_to_all(blocks, PEERS, split_axis=0, concat_axis=0, tiled=True)  14.7 us
    all_to_all x1, waiting for transfers between devices, exchange(): lax.all_to_all(blocks, PEERS, split_axis=0, concat_axis=0, tiled=True)  11.4 us
    all_to_all x1, starting transfers between devices, exchange(): lax.all_to_all(blocks, PEERS, split_axis=0, concat_axis=0, tiled=True)  10.7 us
    pallas_call x5, Pallas kernels, local_call(): pl.pallas_call(kernel, out_shape=outs, in_specs=specs or [VMEM] * len(ope...  8.7 us
    ppermute x1, waiting for transfers between devices, shards(): other = lax.ppermute(total.astype(BF16), 'yh', SWAP)  4.97 us
    ppermute x1, waiting for transfers between devices, shards(): total = total + lax.ppermute(total.astype(BF16), 'xh', SWAP).astype(F32)  2.87 us
    ppermute x1, starting transfers between devices, shards(): total = total + lax.ppermute(total.astype(BF16), 'xh', SWAP).astype(F32)  2.81 us
    ppermute x1, waiting for transfers between devices, shards(): total = total + lax.ppermute(sent, 'c', SWAP).astype(F32)  1.22 us
  transfers between devices with their start and end apart: 4, of which 4 were waited for; matrix products, arithmetic and copies ran while one was open for 0% of the time, Pallas kernels for 1%

profile of v1, /device:TPU:16, one launch (start us, length us, event | category | flops | bytes accessed | tf_op | source)
XLA Modules:
  0.0 59.7 jit_solution(13420631321441113554)
XLA Ops:
  0.6 2.8 %shard_map.86 = bf16[1024,128]{1,0:T(8,128)(2,1)} custom-call(bf16[256,512]{1,0:T(8,128)(2,1)} %bitcast.19, bf16[512,512]{1,0:T(8,128)(2,1)} %constant.4.clone.table_hbm), custom_call_target="tpu_custom_call" | custom-call | flops 134217728 | bytes 786432 | tf_op jit(solution)/shard_map/pallas_call | solution.py:240
  3.5 0.0 copy-start.5
  3.5 0.0 copy-start.3
  3.5 10.7 %all-to-all-start = ((bf16[32,32,128]{2,1,0:T(8,128)(2,1)}), bf16[32,32,128]{2,1,0:T(8,128)(2,1)S(1)}, u32[]{:S(2)}, u32[]{:S(2)}) async-start(bf16[32,32,128]{2,1,0:T(8,128)(2,1)} %bitcast.26), calls=%async_computation | async-start | bytes 524288 | tf_op jit(solution)/shard_map/all_to_all | solution.py:258
  14.2 0.0 copy-done.5
  14.2 0.0 copy-start.4
  14.2 0.1 pad_maximum_fusion.weights_ref
  14.3 0.0 copy-done.3
  14.3 0.6 %copy-done.4 = s32[256,2,8]{0,2,1:T(8,128)S(1)} copy-done((s32[256,2,8]{0,2,1:T(8,128)S(1)}, s32[256,2,8]{0,2,1:T(8,128)}, u32[]{:S(2)}) %copy-start.4) | copy-done | bytes 16408
  14.9 0.0 copy-start.2
  14.9 0.7 %shard_map.87 = (bf16[8,32,128]{2,1,0:T(8,128)(2,1)S(1)}, bf16[8,256,256]{2,1,0:T(8,128)(2,1)S(1)}) custom-call(s32[16,256]{1,0:T(8,128)S(1)} %bitcast.25, s32[128,256]{1,0:T(8,128)S(1)} %bitcast.24), custom_call_target="tpu_custom_call" | custom-call | flops 134217728 | bytes 147456 | tf_op jit(solution)/shard_map/pallas_call | solution.py:240
  15.6 11.4 %all-to-all-done = bf16[32,32,128]{2,1,0:T(8,128)(2,1)S(1)} async-done(((bf16[32,32,128]{2,1,0:T(8,128)(2,1)}), bf16[32,32,128]{2,1,0:T(8,128)(2,1)S(1)}, u32[]{:S(2)}, u32[]{:S(2)}) %all-to-all-start) | async-done | bytes 262176 | tf_op jit(solution)/shard_map/all_to_all | solution.py:258
  27.1 0.0 copy-done.2
  27.1 1.7 %shard_map.88 = (f32[8,24,128]{2,1,0:T(8,128)S(1)}, bf16[8,24,128]{2,1,0:T(8,128)(2,1)S(1)}) custom-call(bf16[1024,128]{1,0:T(8,128)(2,1)S(1)} %bitcast.21, bf16[8,256,256]{2,1,0:T(8,128)(2,1)S(1)} %get-tuple-element.9.y_ref, bf16[8,32,128]{2,1,0:T(8,128)(2,1)S(1)} %get-tuple-element.10.x_ref, f32[16,128]{1,0:T(8,128)S(1)} %bitcast.23, ...), custom_call_target="tpu_custom_call" | custom-call | flops 134217728 | bytes 1388544 | tf_op jit(solution)/shard_map/pallas_call | solution.py:240
  28.8 0.1 collective-permute-start
  28.9 1.2 %collective-permute-done = bf16[8,24,128]{2,1,0:T(8,128)(2,1)S(1)} collective-permute-done((bf16[8,24,128]{2,1,0:T(8,128)(2,1)S(1)}, bf16[8,24,128]{2,1,0:T(8,128)(2,1)S(1)}, u32[]{:S(2)}, u32[]{:S(2)}) %collective-permute-start) | collective-permute-done | bytes 49184 | tf_op jit(solution)/shard_map/ppermute | solution.py:312
  30.2 2.8 %collective-permute-start.1 = (bf16[8,24,128]{2,1,0:T(8,128)(2,1)S(1)}, bf16[8,24,128]{2,1,0:T(8,128)(2,1)S(1)}, u32[]{:S(2)}, u32[]{:S(2)}) collective-permute-start(bf16[8,24,128]{2,1,0:T(8,128)(2,1)S(1)} %fusion), channel_id=1, source_target_pairs={{0,2},{2,0},{1,3},{3,1},{4,6},{6,4},{5,7},{7,5},{8,10},{10,8},{9,1... | collective-permute-start | bytes 147464 | tf_op jit(solution)/shard_map/ppermute | solution.py:313
  33.0 2.9 %collective-permute-done.1 = bf16[8,24,128]{2,1,0:T(8,128)(2,1)S(1)} collective-permute-done((bf16[8,24,128]{2,1,0:T(8,128)(2,1)S(1)}, bf16[8,24,128]{2,1,0:T(8,128)(2,1)S(1)}, u32[]{:S(2)}, u32[]{:S(2)}) %collective-permute-start.1) | collective-permute-done | bytes 49184 | tf_op jit(solution)/shard_map/ppermute | solution.py:313
  35.9 0.7 %collective-permute-start.2 = (bf16[8,24,128]{2,1,0:T(8,128)(2,1)S(1)}, bf16[8,24,128]{2,1,0:T(8,128)(2,1)S(1)}, u32[]{:S(2)}, u32[]{:S(2)}) collective-permute-start(bf16[8,24,128]{2,1,0:T(8,128)(2,1)S(1)} %get-tuple-element.16), channel_id=1, source_target_pairs={{0,128},{128,0},{1,129},{129,1},{2,130},{130,2},{3,131},{131,3},{4... | collective-permute-start | bytes 147464 | tf_op jit(solution)/shard_map/ppermute | solution.py:314
  36.6 5.0 %collective-permute-done.2.other_ref = bf16[8,24,128]{2,1,0:T(8,128)(2,1)S(1)} collective-permute-done((bf16[8,24,128]{2,1,0:T(8,128)(2,1)S(1)}, bf16[8,24,128]{2,1,0:T(8,128)(2,1)S(1)}, u32[]{:S(2)}, u32[]{:S(2)}) %collective-permute-start.2) | collective-permute-done | bytes 49184 | tf_op jit(solution)/shard_map/ppermute | solution.py:314
  41.5 0.0 copy-start.1
  41.6 2.4 %shard_map.89 = (f32[16,128]{1,0:T(8,128)}, bf16[1024,128]{1,0:T(8,128)(2,1)S(1)}) custom-call(f32[8,24,128]{2,1,0:T(8,128)S(1)} %get-tuple-element.17.sum_ref, bf16[8,24,128]{2,1,0:T(8,128)(2,1)S(1)} %collective-permute-done.2.other_ref, bf16[8,256,256]{2,1,0:T(8,128)(2,1)S(1)} %get-tuple-element.9.y_ref, bf16[8,32,128]{2,1,0:T(8,128)(2,1)S(1)} %get-tuple-element.10.x_ref), custom_call_target="tpu_custom_call" | custom-call | flops 134217728 | bytes 1261568 | tf_op jit(solution)/shard_map/pallas_call | solution.py:240
  43.9 0.0 copy-start
  44.0 14.7 %all_to_all.10 = bf16[32,32,128]{2,1,0:T(8,128)(2,1)S(1)} all-to-all(bf16[32,32,128]{2,1,0:T(8,128)(2,1)S(1)} %bitcast.22), channel_id=1, replica_groups=mesh['yh'=2,'yl'=2,'zl'=4,'c'=2,'zh'=2,'xh'=2,'xl'=2] {'yl','zl','zh','xl'}, dimensions={0} | all-to-all | bytes 524288 | tf_op jit(solution)/shard_map/all_to_all | solution.py:258
  58.7 0.0 copy-done.1
  58.7 0.0 copy-done
  58.7 1.0 %shard_map.90 = bf16[256,512]{1,0:T(8,128)(2,1)} custom-call(bf16[1024,128]{1,0:T(8,128)(2,1)S(1)} %bitcast.18, bf16[256,512]{1,0:T(8,128)(2,1)S(1)} %bitcast.20, bf16[512,512]{1,0:T(8,128)(2,1)S(1)} %copy-done.1), custom_call_target="tpu_custom_call" | custom-call | flops 134217728 | bytes 1048576 | tf_op jit(solution)/shard_map/pallas_call | solution.py:240
  (3 shorter events, 0.0 us)
Async XLA Ops:
  3.5 10.7 %copy-start.5 = (f32[1,16,64]{2,1,0:T(8,128)S(1)}, f32[1,16,64]{2,1,0:T(8,128)}, u32[]{:S(2)}) copy-start(f32[1,16,64]{2,1,0:T(8,128)} %param.11) | copy-start | bytes 12292
  3.5 10.8 %copy-start.3 = (s32[256,2,64]{0,2,1:T(8,128)S(1)}, s32[256,2,64]{0,2,1:T(8,128)}, u32[]{:S(2)}) copy-start(s32[256,2,64]{0,2,1:T(8,128)} %param.9) | copy-start | bytes 393220
  3.5 23.6 %all-to-all-start = ((bf16[32,32,128]{2,1,0:T(8,128)(2,1)}), bf16[32,32,128]{2,1,0:T(8,128)(2,1)S(1)}, u32[]{:S(2)}, u32[]{:S(2)}) async-start(bf16[32,32,128]{2,1,0:T(8,128)(2,1)} %bitcast.26), calls=%async_computation | async-start | bytes 524288 | tf_op jit(solution)/shard_map/all_to_all | solution.py:258
  14.2 0.7 %copy-start.4 = (s32[256,2,8]{0,2,1:T(8,128)S(1)}, s32[256,2,8]{0,2,1:T(8,128)}, u32[]{:S(2)}) copy-start(s32[256,2,8]{0,2,1:T(8,128)} %param.8) | copy-start | bytes 49156
  14.9 12.2 %copy-start.2 = (f32[1,16,128]{2,1,0:T(8,128)S(1)}, f32[1,16,128]{2,1,0:T(8,128)}, u32[]{:S(2)}) copy-start(f32[1,16,128]{2,1,0:T(8,128)} %param.10) | copy-start | bytes 24580
  28.8 1.3 %collective-permute-start = (bf16[8,24,128]{2,1,0:T(8,128)(2,1)S(1)}, bf16[8,24,128]{2,1,0:T(8,128)(2,1)S(1)}, u32[]{:S(2)}, u32[]{:S(2)}) collective-permute-start(bf16[8,24,128]{2,1,0:T(8,128)(2,1)S(1)} %get-tuple-element.13), channel_id=1, source_target_pairs={{0,8},{8,0},{1,9},{9,1},{2,10},{10,2},{3,11},{11,3},{4,12},{12,4},... | collective-permute-start | bytes 147464 | tf_op jit(solution)/shard_map/ppermute | solution.py:312
  30.2 5.7 %collective-permute-start.1 = (bf16[8,24,128]{2,1,0:T(8,128)(2,1)S(1)}, bf16[8,24,128]{2,1,0:T(8,128)(2,1)S(1)}, u32[]{:S(2)}, u32[]{:S(2)}) collective-permute-start(bf16[8,24,128]{2,1,0:T(8,128)(2,1)S(1)} %fusion), channel_id=1, source_target_pairs={{0,2},{2,0},{1,3},{3,1},{4,6},{6,4},{5,7},{7,5},{8,10},{10,8},{9,1... | collective-permute-start | bytes 147464 | tf_op jit(solution)/shard_map/ppermute | solution.py:313
  35.9 5.7 %collective-permute-start.2 = (bf16[8,24,128]{2,1,0:T(8,128)(2,1)S(1)}, bf16[8,24,128]{2,1,0:T(8,128)(2,1)S(1)}, u32[]{:S(2)}, u32[]{:S(2)}) collective-permute-start(bf16[8,24,128]{2,1,0:T(8,128)(2,1)S(1)} %get-tuple-element.16), channel_id=1, source_target_pairs={{0,128},{128,0},{1,129},{129,1},{2,130},{130,2},{3,131},{131,3},{4... | collective-permute-start | bytes 147464 | tf_op jit(solution)/shard_map/ppermute | solution.py:314
  41.5 17.1 %copy-start.1 = (bf16[512,512]{1,0:T(8,128)(2,1)S(1)}, bf16[512,512]{1,0:T(8,128)(2,1)}, u32[]{:S(2)}) copy-start(bf16[512,512]{1,0:T(8,128)(2,1)} %constant.5.clone.table_ref) | copy-start | bytes 1572868
  43.9 14.7 %copy-start = (bf16[8,32,512]{2,1,0:T(8,128)(2,1)S(1)}, bf16[8,32,512]{2,1,0:T(8,128)(2,1)}, u32[]{:S(2)}) copy-start(bf16[8,32,512]{2,1,0:T(8,128)(2,1)} %param.7) | copy-start | bytes 786436

commit v2 on v1

v2 whole, which is shorter than its diff:
```python
import functools
import math

import jax
import jax.numpy as jnp
import numpy as np
from jax import lax
from jax.experimental import pallas as pl
from jax.experimental.pallas import tpu as pltpu
from jax.sharding import Mesh
from jax.sharding import PartitionSpec as P

FINE = 4096
GRAIN = 32
LANES = 128
VMEM_LIMIT = 12 * 2**20
F32 = jnp.float32
BF16 = jnp.bfloat16
AXES = {"y": 4, "zl": 4, "c": 2, "zh": 2, "x": 4}
SLAB = ("y", "zl", "c")
ROWS = ("zh", "x")
PEERS = ("zl", "y", "x", "zh")
TEAM = ("c",)
PLANES = 2
SWAP = [(0, 1), (1, 0)]


def plane_of(**at):
    number = 0
    for axis in SLAB + ROWS:
        number = number * AXES[axis] + at[axis]
    return number


def column_table(length, scale):
    grid = np.arange(length // 2).reshape([AXES[a] for a in SLAB + ROWS])
    order = grid.transpose([(SLAB + ROWS).index(a) for a in PEERS + TEAM]).reshape(-1)
    depths = np.arange(length, dtype=np.int64)
    angles = (order[:, None] * depths[None, :] % length) * (2.0 * math.pi / length)
    matrix = np.stack([np.cos(angles), -np.sin(angles)], axis=1) * scale
    return matrix.reshape(length, length).astype(np.float32).astype(BF16)


def cosine_of_turns(turns):
    part = turns - jnp.floor(turns + 0.5)
    angle = (0.25 - jnp.abs(part)) * (2.0 * math.pi)
    square = angle * angle
    series = -1.0 / 39916800.0
    for term in (362880.0, -5040.0, 120.0, -6.0):
        series = series * square + 1.0 / term
    return angle + angle * square * series


def dot(left, right, left_dim, right_dim):
    dims = (((left_dim,), (right_dim,)), ((), ()))
    return lax.dot_general(left, right, dims, preferred_element_type=F32)


def iota(shape, axis):
    return lax.broadcasted_iota(jnp.int32, shape, axis)


def exchange_grains(blocks):
    lane = iota(blocks[0].shape, 1)
    low = lane < 2 * GRAIN
    even = (lane & GRAIN) == 0
    first = [None] * 4
    for i in (0, 1):
        a, b = blocks[i], blocks[i + 2]
        first[i] = jnp.where(low, a, pltpu.roll(b, 2 * GRAIN, 1))
        first[i + 2] = jnp.where(low, pltpu.roll(a, 2 * GRAIN, 1), b)
    last = [None] * 4
    for i in (0, 2):
        a, b = first[i], first[i + 1]
        last[i] = jnp.where(even, a, pltpu.roll(b, GRAIN, 1))
        last[i + 1] = jnp.where(even, pltpu.roll(a, 3 * GRAIN, 1), b)
    return last


def forward_kernel(scale, out_ref):
    length = out_ref.shape[1]
    low = (32, length)
    row, depth = iota(low, 0), iota(low, 1)
    plane = ((row >> 1) & 1) * 8 + ((row >> 2) & 1) * 4 + (row >> 3)
    low_real = (plane * depth).astype(F32) * (1.0 / length) + (row & 1).astype(F32) * 0.25
    low_real, low_imag = cosine_of_turns(low_real), cosine_of_turns(low_real + 0.25)
    row, depth = iota((16, length), 0), iota((16, length), 1)
    plane = ((row & 3) * 4 + (row >> 2)) * 16
    high = (plane * depth).astype(F32) * (1.0 / length)
    high_real, high_imag = cosine_of_turns(high) * scale, cosine_of_turns(high + 0.25) * scale
    for b in range(16):
        real, imag = high_real[b : b + 1], high_imag[b : b + 1]
        out_ref[pl.ds(b * 32, 32), :] = (real * low_real - imag * low_imag).astype(BF16)


def tables_kernel(x_ref, y_ref, after_ref, x_table_ref, y_table_ref, turned):
    at = {a: lax.axis_index(a) for a in SLAB + ROWS}
    turned[...] = y_ref[...].astype(F32).T
    x_all = x_ref[...].astype(F32)
    lane_plane = iota(x_all.shape, 1)
    shape = (32, 4 * LANES)
    lane = iota(shape, 1)
    x_at = ((lane >> 3) & 1) * 32 + ((lane >> 4) & 3) * 8 + ((lane >> 2) & 1) * 4
    x_at = (x_at + ((lane >> 6) & 3)).astype(F32)
    quarter = 3 * ((lane >> 8) + (lane & 1)) + (iota(shape, 0) >> 4)
    x_shift = (quarter * (FINE // 4)).astype(F32)
    team = (lane >> 1) & 1
    y_in = iota((32, LANES), 0).astype(F32)
    y_block = (iota((16, LANES), 0) * 64 + at["c"] * 32).astype(F32)
    for p in range(PLANES):
        plane = plane_of(**{**at, "c": p})
        kx = jnp.sum(jnp.where(lane_plane == plane, x_all, 0.0), axis=1, keepdims=True)
        kx = jnp.concatenate([kx, kx], axis=0) + FINE / 2.0
        phase = cosine_of_turns((kx * x_at + x_shift) * (1.0 / FINE))
        x_table_ref[p] = jnp.where(team == p, phase, 0.0).astype(BF16)
        ky = (turned[pl.ds(plane, 1), :] + FINE / 2.0) * (1.0 / FINE)
        fine = ky * y_in
        fine_real, fine_imag = cosine_of_turns(fine), cosine_of_turns(fine + 0.25)
        coarse = ky * y_block
        coarse_real, coarse_imag = cosine_of_turns(coarse), cosine_of_turns(coarse + 0.25)
        for b in range(16):
            real, imag = coarse_real[b : b + 1], coarse_imag[b : b + 1]
            rows = pl.ds(b * 32, 32)
            near, far = pl.ds(2 * p * LANES, LANES), pl.ds((2 * p + 1) * LANES, LANES)
            y_table_ref[rows, near] = (real * fine_real - imag * fine_imag).astype(BF16)
            y_table_ref[rows, far] = (real * fine_imag + imag * fine_real).astype(BF16)


def transform_kernel(columns_ref, table_ref, out_ref):
    spectrum = dot(table_ref[...], columns_ref[...], 1, 1)
    pairs = spectrum.shape[0] // 8
    near = spectrum[:, :LANES].reshape(pairs, 8, LANES)
    far = spectrum[:, LANES:].reshape(pairs, 8, LANES)
    low = iota(near.shape, 1) < 4
    even = jnp.where(low, near, pltpu.roll(far, 4, 1))
    odd = jnp.where(low, pltpu.roll(near, 4, 1), far)
    out_ref[...] = jnp.concatenate([even, odd], axis=1).reshape(out_ref.shape).astype(BF16)


def predict_kernel(scale, planes_ref, y_ref, x_ref, measured_ref, weights_ref, out_ref):
    quarter = planes_ref.shape[0] // 4
    blocks = [planes_ref[pl.ds(g * quarter, quarter), :].astype(F32) for g in range(4)]
    blocks = exchange_grains(blocks)
    rows = quarter // 4
    left = jnp.concatenate(
        [
            jnp.concatenate([b[i * rows : i * rows + rows] for b in blocks], axis=0)
            for i in range(4)
        ],
        axis=1,
    ).astype(BF16)
    inner = dot(left, y_ref[...], 1, 0).astype(BF16)
    first = iota((8, LANES), 1) < LANES // 2
    for p in range(PLANES):
        near = inner[:, 2 * p * LANES : (2 * p + 1) * LANES]
        far = inner[:, (2 * p + 1) * LANES : (2 * p + 2) * LANES]
        points = dot(x_ref[p], jnp.concatenate([near, far], axis=0), 1, 0) * scale
        real, imag = points[:16], points[16:]
        out_ref[p, :8] = jnp.where(first, real[:8], pltpu.roll(imag[:8], 64, 1))
        out_ref[p, 8:16] = jnp.where(first, pltpu.roll(real[8:], 64, 1), imag[8:])
        out_ref[p, 16:] = jnp.zeros((16, LANES), F32)
    own = lax.axis_index("c")
    out_ref[own, :16] = out_ref[own, :16] - measured_ref[...]
    out_ref[own, 16:, : LANES // 2] = weights_ref[...]


def spread_kernel(scale, mine_ref, other_ref, y_ref, x_ref, misfit_ref, out_ref):
    first = iota((8, LANES), 1) < LANES // 2
    zero = jnp.zeros((8, LANES), F32)

    def both(weight):
        return jnp.where(first, weight, pltpu.roll(weight, 64, 1))

    def misfit_of(total):
        return total[:8] * both(total[16:24]), total[8:16] * both(total[24:])

    pieces = []
    for p in range(PLANES):
        near, far = misfit_of(mine_ref[p] + other_ref[p])
        spread = jnp.concatenate(
            [
                jnp.where(first, near, zero),
                jnp.where(first, zero, pltpu.roll(far, 64, 1)),
                jnp.where(first, pltpu.roll(near, 64, 1), zero),
                jnp.where(first, zero, far),
            ],
            axis=0,
        ).astype(BF16)
        inner = dot(x_ref[p], spread, 0, 0).astype(BF16)
        half = inner.shape[0] // 2
        pieces += [inner[:half], inner[half:]]
    planes = dot(jnp.concatenate(pieces, axis=1), y_ref[...], 1, 1) * scale
    rows = planes.shape[0] // 4
    for i in range(4):
        lanes = slice(i * LANES, i * LANES + LANES)
        blocks = [planes[q * rows : q * rows + rows, lanes] for q in range(4)]
        blocks = exchange_grains(blocks)
        for g in range(4):
            out_ref[pl.ds((4 * g + i) * rows, rows), :] = blocks[g].astype(BF16)
    own = lax.axis_index("c")
    near, far = misfit_of(mine_ref[own] + other_ref[own])
    misfit_ref[:8], misfit_ref[8:] = near, far


def update_kernel(planes_ref, columns_ref, table_ref, out_hbm, staged, sems):
    planes = planes_ref[...].astype(F32)
    planes = planes.reshape(planes.shape[0] // 16, 16, LANES)
    even, odd = planes[:, :8], planes[:, 8:]
    low = iota(even.shape, 1) < 4
    near = jnp.where(low, even, pltpu.roll(odd, 4, 1)).reshape(-1, LANES).astype(BF16)
    far = jnp.where(low, pltpu.roll(even, 4, 1), odd).reshape(-1, LANES).astype(BF16)
    table = table_ref[...]
    stores = []
    for i, back in enumerate((near, far)):
        part = pl.ds(i * LANES, LANES)
        correction = dot(back, table, 0, 0)
        staged[part, :] = (columns_ref[part, :].astype(F32) - 0.5 * correction).astype(BF16)
        stores.append(pltpu.make_async_copy(staged.at[part], out_hbm.at[part], sems.at[i]))
        stores[-1].start()
    for store in stores:
        store.wait()


VMEM = pl.BlockSpec(memory_space=pltpu.VMEM)
ANY = pl.BlockSpec(memory_space=pl.ANY)


def local_call(kernel, outs, operands, scratch=(), specs=None, out_specs=None, flops=2**27):
    return pl.pallas_call(
        kernel,
        out_shape=outs,
        in_specs=specs or [VMEM] * len(operands),
        out_specs=jax.tree.map(lambda _: VMEM, outs) if out_specs is None else out_specs,
        scratch_shapes=scratch,
        compiler_params=pltpu.CompilerParams(vmem_limit_bytes=VMEM_LIMIT),
        cost_estimate=pl.CostEstimate(flops=flops, bytes_accessed=flops // 128, transcendentals=0),
    )(*operands)


def shape_of(*shape, dtype=BF16):
    return jax.ShapeDtypeStruct(shape, dtype)


def exchange(array):
    peers = math.prod(AXES[a] for a in PEERS)
    blocks = array.reshape(peers, array.shape[0] // peers, array.shape[1])
    blocks = lax.all_to_all(blocks, PEERS, split_axis=0, concat_axis=0, tiled=True)
    return blocks.reshape(array.shape)


def shards(volume, x_frequency, y_frequency, measured, weights):
    x_local, y_local, length = volume.shape
    cells = x_local * y_local
    rows = cells * length // LANES
    planes, angles, kx_count = x_frequency.shape
    ky_count = y_frequency.shape[2]
    forward_scale = 1.0 / math.sqrt(cells * math.prod(AXES.values()))
    back_scale = 1.0 / math.sqrt(angles * kx_count * ky_count)
    columns = volume.reshape(cells, length)
    forward = local_call(
        functools.partial(forward_kernel, 1.0 / math.sqrt(length)),
        shape_of(length, length),
        (),
        flops=2**10,
    )
    inverse = column_table(length, 1.0 / math.sqrt(planes))

    sending = local_call(
        transform_kernel,
        shape_of(rows, LANES),
        (columns, forward),
    )
    x_table, y_table = local_call(
        tables_kernel,
        (shape_of(PLANES, 32, 4 * LANES), shape_of(4 * LANES, 4 * LANES)),
        (
            x_frequency.transpose(1, 2, 0).reshape(angles * kx_count, planes),
            y_frequency.transpose(1, 2, 0).reshape(angles * ky_count, planes),
            sending,
        ),
        [pltpu.VMEM((planes, LANES), F32)],
        [VMEM, VMEM, ANY],
        flops=2**10,
    )
    x_table, y_table, sending = lax.optimization_barrier((x_table, y_table, sending))
    received = exchange(sending)
    points = local_call(
        functools.partial(predict_kernel, forward_scale),
        shape_of(PLANES, 32, LANES, dtype=F32),
        (received, y_table, x_table, measured[0], weights[0]),
    )
    others = lax.ppermute(points, "c", SWAP)
    misfit, sending = local_call(
        functools.partial(spread_kernel, back_scale),
        (shape_of(angles * kx_count, LANES, dtype=F32), shape_of(rows, LANES)),
        (points, others, y_table, x_table),
    )
    received = exchange(sending)
    updated = local_call(
        update_kernel,
        shape_of(cells, length),
        (received, columns, inverse),
        [pltpu.VMEM((cells, length), BF16), pltpu.SemaphoreType.DMA((2,))],
        out_specs=ANY,
    )
    return (updated.reshape(volume.shape), misfit.reshape(measured.shape))


def solution(mesh):
    fine = Mesh(mesh.devices.reshape(tuple(AXES.values())), tuple(AXES))
    placed = (
        P(ROWS, SLAB, None),
        P(),
        P(),
        P(SLAB + ROWS, None, None),
        P(SLAB + ROWS, None, None),
    )
    return jax.shard_map(
        shards,
        mesh=fine,
        in_specs=placed,
        out_specs=(P(ROWS, SLAB, None), P(SLAB + ROWS, None, None)),
        check_vma=False,
    )
```

time: 60 us -> 57.1 us (0.952)
  the two profiles are of different devices: /device:TPU:16 before, /device:TPU:32 now
where the time goes in v2:
time: 57.1 us; the launch traced here: 56.9 us
  blocking collectives  49.7 us (87%)
  Pallas kernels  3.98 us (7%)
  local copies, waits for them, and re-layouts  1.21 us (2%)
  waiting for transfers between devices  1.19 us (2%)
  between operations  0.69 us (1%)
    all_to_all x2, blocking collectives, exchange(): lax.all_to_all(blocks, PEERS, split_axis=0, concat_axis=0, tiled=True)  49.7 us
    pallas_call x6, Pallas kernels, local_call(): pl.pallas_call(kernel, out_shape=outs, in_specs=specs or [VMEM] * len(ope...  3.98 us
    unnamed x12, local copies, waits for them, and re-layouts  1.21 us
    ppermute x1, waiting for transfers between devices, shards(): others = lax.ppermute(points, 'c', SWAP)  1.19 us
  transfers between devices with their start and end apart: 1, of which 1 were waited for; matrix products, arithmetic and copies ran while one was open for 0% of the time, Pallas kernels for 0%

profile of v2, /device:TPU:32, one launch (start us, length us, event | category | flops | bytes accessed | tf_op | source)
XLA Modules:
  0.0 56.9 jit_solution(11001934834791098749)
XLA Ops:
  0.6 0.0 copy-start
  0.6 0.3 shard_map.77.table_ref
  1.0 0.6 %copy-done = bf16[8,32,512]{2,1,0:T(8,128)(2,1)S(1)} copy-done((bf16[8,32,512]{2,1,0:T(8,128)(2,1)S(1)}, bf16[8,32,512]{2,1,0:T(8,128)(2,1)}, u32[]{:S(2)}) %copy-start) | copy-done | bytes 262168
  1.6 0.0 copy-start.2
  1.6 0.0 copy-start.3
  1.6 0.3 shard_map.78.after_ref
  1.9 0.6 copy-done.2
  2.5 0.0 copy-done.3
  2.5 0.5 shard_map.79
  3.0 0.0 copy-start.4
  3.0 0.0 copy-start.5
  3.0 28.9 %all_to_all.10 = bf16[128,8,128]{2,1,0:T(8,128)(2,1)S(1)} all-to-all(bf16[128,8,128]{2,1,0:T(8,128)(2,1)S(1)} %bitcast.15), channel_id=1, replica_groups=mesh['y'=4,'zl'=4,'c'=2,'zh'=2,'x'=4] {'zl','y','x','zh'}, dimensions={0} | all-to-all | bytes 524288 | tf_op jit(solution)/shard_map/all_to_all | solution.py:247
  31.9 0.0 copy-done.4
  31.9 0.0 copy-done.5
  31.9 0.7 %shard_map.80.mine_ref = f32[2,32,128]{2,1,0:T(8,128)S(1)} custom-call(bf16[1024,128]{1,0:T(8,128)(2,1)S(1)} %bitcast.17, bf16[512,512]{1,0:T(8,128)(2,1)S(1)} %get-tuple-element.12.y_ref, bf16[2,32,512]{2,1,0:T(8,128)(2,1)S(1)} %get-tuple-element.13.x_ref, f32[16,128]{1,0:T(8,128)S(1)} %bitcast.23, f32[16,64]{1,0:T(8,128)S(1)} %bitcast.24), custom_call_target="tpu_custom_call" | custom-call | flops 134217728 | bytes 1048576 | tf_op jit(solution)/shard_map/pallas_call | solution.py:229
  32.6 0.0 copy-start.1
  32.6 0.1 collective-permute-start
  32.7 1.2 %collective-permute-done.other_ref = f32[2,32,128]{2,1,0:T(8,128)S(1)} collective-permute-done((f32[2,32,128]{2,1,0:T(8,128)S(1)}, f32[2,32,128]{2,1,0:T(8,128)S(1)}, u32[]{:S(2)}, u32[]{:S(2)}) %collective-permute-start) | collective-permute-done | bytes 32800 | tf_op jit(solution)/shard_map/ppermute | solution.py:292
  33.9 1.1 %shard_map.81 = (f32[16,128]{1,0:T(8,128)}, bf16[1024,128]{1,0:T(8,128)(2,1)S(1)}) custom-call(f32[2,32,128]{2,1,0:T(8,128)S(1)} %shard_map.80.mine_ref, f32[2,32,128]{2,1,0:T(8,128)S(1)} %collective-permute-done.other_ref, bf16[512,512]{1,0:T(8,128)(2,1)S(1)} %get-tuple-element.12.y_ref, bf16[2,32,512]{2,1,0:T(8,128)(2,1)S(1)} %get-tuple-element.13.x_ref), custom_call_target="tpu_custom_call" | custom-call | flops 134217728 | bytes 1048576 | tf_op jit(solution)/shard_map/pallas_call | solution.py:229
  35.0 20.8 %all_to_all.11 = bf16[128,8,128]{2,1,0:T(8,128)(2,1)S(1)} all-to-all(bf16[128,8,128]{2,1,0:T(8,128)(2,1)S(1)} %bitcast.20), channel_id=1, replica_groups=mesh['y'=4,'zl'=4,'c'=2,'zh'=2,'x'=4] {'zl','y','x','zh'}, dimensions={0} | all-to-all | bytes 524288 | tf_op jit(solution)/shard_map/all_to_all | solution.py:247
  55.8 0.0 copy-done.1
  55.8 1.0 %shard_map.82 = bf16[256,512]{1,0:T(8,128)(2,1)} custom-call(bf16[1024,128]{1,0:T(8,128)(2,1)S(1)} %bitcast.16, bf16[256,512]{1,0:T(8,128)(2,1)S(1)} %bitcast.19, bf16[512,512]{1,0:T(8,128)(2,1)S(1)} %copy-done.1), custom_call_target="tpu_custom_call" | custom-call | flops 134217728 | bytes 1048576 | tf_op jit(solution)/shard_map/pallas_call | solution.py:229
Async XLA Ops:
  0.6 1.0 %copy-start = (bf16[8,32,512]{2,1,0:T(8,128)(2,1)S(1)}, bf16[8,32,512]{2,1,0:T(8,128)(2,1)}, u32[]{:S(2)}) copy-start(bf16[8,32,512]{2,1,0:T(8,128)(2,1)} %param.6) | copy-start | bytes 786436
  1.6 0.9 %copy-start.2 = (s32[256,2,64]{0,2,1:T(8,128)S(1)}, s32[256,2,64]{0,2,1:T(8,128)}, u32[]{:S(2)}) copy-start(s32[256,2,64]{0,2,1:T(8,128)} %param.8) | copy-start | bytes 393220
  1.6 0.9 %copy-start.3 = (s32[256,2,8]{0,2,1:T(8,128)S(1)}, s32[256,2,8]{0,2,1:T(8,128)}, u32[]{:S(2)}) copy-start(s32[256,2,8]{0,2,1:T(8,128)} %param.7) | copy-start | bytes 49156
  3.0 28.9 %copy-start.4 = (f32[1,16,128]{2,1,0:T(8,128)S(1)}, f32[1,16,128]{2,1,0:T(8,128)}, u32[]{:S(2)}) copy-start(f32[1,16,128]{2,1,0:T(8,128)} %param.9) | copy-start | bytes 24580
  3.0 28.9 %copy-start.5 = (f32[1,16,64]{2,1,0:T(8,128)S(1)}, f32[1,16,64]{2,1,0:T(8,128)}, u32[]{:S(2)}) copy-start(f32[1,16,64]{2,1,0:T(8,128)} %param.10) | copy-start | bytes 12292
  32.6 23.2 %copy-start.1 = (bf16[512,512]{1,0:T(8,128)(2,1)S(1)}, bf16[512,512]{1,0:T(8,128)(2,1)}, u32[]{:S(2)}) copy-start(bf16[512,512]{1,0:T(8,128)(2,1)} %constant.2.clone.table_ref) | copy-start | bytes 1572868
  32.6 1.3 %collective-permute-start = (f32[2,32,128]{2,1,0:T(8,128)S(1)}, f32[2,32,128]{2,1,0:T(8,128)S(1)}, u32[]{:S(2)}, u32[]{:S(2)}) collective-permute-start(f32[2,32,128]{2,1,0:T(8,128)S(1)} %shard_map.80.mine_ref), channel_id=1, source_target_pairs={{0,8},{8,0},{1,9},{9,1},{2,10},{10,2},{3,11},{11,3},{4,12},{12,4},... | collective-permute-start | bytes 98312 | tf_op jit(solution)/shard_map/ppermute | solution.py:292

commit v3 on v2

--- a/solution.py
+++ b/solution.py
@@ -14,15 +14,50 @@
 GRAIN = 32
 LANES = 128
 VMEM_LIMIT = 12 * 2**20
+START_LIMIT = 12 * 2**20
 F32 = jnp.float32
 BF16 = jnp.bfloat16
 AXES = {"y": 4, "zl": 4, "c": 2, "zh": 2, "x": 4}
 SLAB = ("y", "zl", "c")
 ROWS = ("zh", "x")
-PEERS = ("zl", "y", "x", "zh")
+OUT = ("zl", "y", "x", "zh")
+BACK = ("zl", "y", "x", "zh")
 TEAM = ("c",)
 PLANES = 2
 SWAP = [(0, 1), (1, 0)]
+
+
+def bits_of(axes):
+    return [
+        (a, 1 << b) for a in axes for b in reversed(range(AXES[a].bit_length() - 1))
+    ]
+
+
+PLANE_STEP = {"y": 64, "zl": 16, "c": 8, "zh": 4, "x": 1}
+X_STEP = {"zh": 32, "x": 8}
+CROSS = tuple(a for a in OUT if a in X_STEP)
+
+
+def weighted(index, steps):
+    total = 0
+    for place, step in enumerate(reversed(steps)):
+        if step:
+            total = total + ((index >> place) & 1) * step
+    return total
+
+
+def runs(peers, **fixed):
+    found = []
+    for at in np.ndindex(*[AXES[a] for a in CROSS]):
+        at = {**fixed, **dict(zip(CROSS, at))}
+        peer = 0
+        for axis in peers:
+            peer = peer * AXES[axis] + at[axis]
+        if found and sum(found[-1]) == peer:
+            found[-1] = (found[-1][0], found[-1][1] + 1)
+        else:
+            found.append((int(peer), 1))
+    return found
 
 
 def plane_of(**at):
@@ -32,9 +67,9 @@
     return number
 
 
-def column_table(length, scale):
+def column_table(length, scale, peers):
     grid = np.arange(length // 2).reshape([AXES[a] for a in SLAB + ROWS])
-    order = grid.transpose([(SLAB + ROWS).index(a) for a in PEERS + TEAM]).reshape(-1)
+    order = grid.transpose([(SLAB + ROWS).index(a) for a in peers + TEAM]).reshape(-1)
     depths = np.arange(length, dtype=np.int64)
     angles = (order[:, None] * depths[None, :] % length) * (2.0 * math.pi / length)
     matrix = np.stack([np.cos(angles), -np.sin(angles)], axis=1) * scale
@@ -77,31 +112,47 @@
     return last
 
 
-def forward_kernel(scale, out_ref):
-    length = out_ref.shape[1]
-    low = (32, length)
-    row, depth = iota(low, 0), iota(low, 1)
-    plane = ((row >> 1) & 1) * 8 + ((row >> 2) & 1) * 4 + (row >> 3)
-    low_real = (plane * depth).astype(F32) * (1.0 / length) + (row & 1).astype(F32) * 0.25
-    low_real, low_imag = cosine_of_turns(low_real), cosine_of_turns(low_real + 0.25)
-    row, depth = iota((16, length), 0), iota((16, length), 1)
-    plane = ((row & 3) * 4 + (row >> 2)) * 16
-    high = (plane * depth).astype(F32) * (1.0 / length)
-    high_real, high_imag = cosine_of_turns(high) * scale, cosine_of_turns(high + 0.25) * scale
-    for b in range(16):
-        real, imag = high_real[b : b + 1], high_imag[b : b + 1]
-        out_ref[pl.ds(b * 32, 32), :] = (real * low_real - imag * low_imag).astype(BF16)
-
-
-def tables_kernel(x_ref, y_ref, after_ref, x_table_ref, y_table_ref, turned):
+def start_kernel(
+    x_hbm,
+    y_hbm,
+    columns_hbm,
+    forward_hbm,
+    measured_hbm,
+    weights_hbm,
+    out_ref,
+    own_ref,
+    x_table_ref,
+    y_table_ref,
+    x_own,
+    y_all,
+    columns,
+    forward,
+    measured,
+    weights,
+    turned,
+    sems,
+):
+    pairs = (
+        (x_hbm, x_own),
+        (y_hbm, y_all),
+        (columns_hbm, columns),
+        (forward_hbm, forward),
+        (measured_hbm, measured),
+        (weights_hbm, weights),
+    )
+    loads = [pltpu.make_async_copy(a, b, sems.at[i]) for i, (a, b) in enumerate(pairs)]
+    for load in loads:
+        load.start()
     at = {a: lax.axis_index(a) for a in SLAB + ROWS}
-    turned[...] = y_ref[...].astype(F32).T
-    x_all = x_ref[...].astype(F32)
+    for load in loads[:2]:
+        load.wait()
+    turned[...] = y_all[...].astype(F32).T
+    x_all = x_own[...].astype(F32)
     lane_plane = iota(x_all.shape, 1)
     shape = (32, 4 * LANES)
     lane = iota(shape, 1)
-    x_at = ((lane >> 3) & 1) * 32 + ((lane >> 4) & 3) * 8 + ((lane >> 2) & 1) * 4
-    x_at = (x_at + ((lane >> 6) & 3)).astype(F32)
+    steps = [X_STEP[a] * value for a, value in bits_of(CROSS)]
+    x_at = weighted(lane, [0, 2, 1] + steps + [4, 0, 0]).astype(F32)
     quarter = 3 * ((lane >> 8) + (lane & 1)) + (iota(shape, 0) >> 4)
     x_shift = (quarter * (FINE // 4)).astype(F32)
     team = (lane >> 1) & 1
@@ -124,10 +175,12 @@
             near, far = pl.ds(2 * p * LANES, LANES), pl.ds((2 * p + 1) * LANES, LANES)
             y_table_ref[rows, near] = (real * fine_real - imag * fine_imag).astype(BF16)
             y_table_ref[rows, far] = (real * fine_imag + imag * fine_real).astype(BF16)
-
-
-def transform_kernel(columns_ref, table_ref, out_ref):
-    spectrum = dot(table_ref[...], columns_ref[...], 1, 1)
+    for load in loads[2:]:
+        load.wait()
+    own_ref[:16] = measured[...]
+    own_ref[16:, LANES // 2 :] = jnp.zeros((16, LANES // 2), F32)
+    own_ref[16:, : LANES // 2] = weights[...]
+    spectrum = dot(forward[...], columns[...], 1, 1)
     pairs = spectrum.shape[0] // 8
     near = spectrum[:, :LANES].reshape(pairs, 8, LANES)
     far = spectrum[:, LANES:].reshape(pairs, 8, LANES)
@@ -137,18 +190,17 @@
     out_ref[...] = jnp.concatenate([even, odd], axis=1).reshape(out_ref.shape).astype(BF16)
 
 
-def predict_kernel(scale, planes_ref, y_ref, x_ref, measured_ref, weights_ref, out_ref):
-    quarter = planes_ref.shape[0] // 4
-    blocks = [planes_ref[pl.ds(g * quarter, quarter), :].astype(F32) for g in range(4)]
-    blocks = exchange_grains(blocks)
-    rows = quarter // 4
-    left = jnp.concatenate(
-        [
-            jnp.concatenate([b[i * rows : i * rows + rows] for b in blocks], axis=0)
-            for i in range(4)
-        ],
-        axis=1,
-    ).astype(BF16)
+def predict_kernel(scale, planes_ref, y_ref, x_ref, own_ref, out_ref):
+    left = []
+    for i in range(4):
+        blocks = []
+        for g in range(4):
+            parts = [
+                planes_ref[pl.ds(8 * peer, 8 * count), :] for peer, count in runs(OUT, zl=g, y=i)
+            ]
+            blocks.append(jnp.concatenate(parts, axis=0))
+        left.append(jnp.concatenate(exchange_grains(blocks), axis=0))
+    left = jnp.concatenate(left, axis=1)
     inner = dot(left, y_ref[...], 1, 0).astype(BF16)
     first = iota((8, LANES), 1) < LANES // 2
     for p in range(PLANES):
@@ -160,8 +212,8 @@
         out_ref[p, 8:16] = jnp.where(first, pltpu.roll(real[8:], 64, 1), imag[8:])
         out_ref[p, 16:] = jnp.zeros((16, LANES), F32)
     own = lax.axis_index("c")
-    out_ref[own, :16] = out_ref[own, :16] - measured_ref[...]
-    out_ref[own, 16:, : LANES // 2] = weights_ref[...]
+    out_ref[own, :16] = out_ref[own, :16] - own_ref[:16]
+    out_ref[own, 16:] = own_ref[16:]
 
 
 def spread_kernel(scale, mine_ref, other_ref, y_ref, x_ref, misfit_ref, out_ref):
@@ -190,13 +242,18 @@
         half = inner.shape[0] // 2
         pieces += [inner[:half], inner[half:]]
     planes = dot(jnp.concatenate(pieces, axis=1), y_ref[...], 1, 1) * scale
+    planes = planes.astype(BF16)
     rows = planes.shape[0] // 4
     for i in range(4):
         lanes = slice(i * LANES, i * LANES + LANES)
         blocks = [planes[q * rows : q * rows + rows, lanes] for q in range(4)]
         blocks = exchange_grains(blocks)
         for g in range(4):
-            out_ref[pl.ds((4 * g + i) * rows, rows), :] = blocks[g].astype(BF16)
+            row = 0
+            for peer, count in runs(BACK, zl=g, y=i):
+                part = blocks[g][row : row + 8 * count]
+                out_ref[pl.ds(8 * peer, 8 * count), :] = part
+                row += 8 * count
     own = lax.axis_index("c")
     near, far = misfit_of(mine_ref[own] + other_ref[own])
     misfit_ref[:8], misfit_ref[8:] = near, far
@@ -223,16 +280,21 @@
 
 VMEM = pl.BlockSpec(memory_space=pltpu.VMEM)
 ANY = pl.BlockSpec(memory_space=pl.ANY)
-
-
-def local_call(kernel, outs, operands, scratch=(), specs=None, out_specs=None, flops=2**27):
+HBM = pl.BlockSpec(memory_space=pltpu.HBM)
+
+
+def pin(array):
+    return pltpu.with_memory_space_constraint(array, pltpu.HBM)
+
+
+def local_call(kernel, outs, operands, scratch=(), specs=None, out_specs=None, flops=2**27, limit=VMEM_LIMIT):
     return pl.pallas_call(
         kernel,
         out_shape=outs,
         in_specs=specs or [VMEM] * len(operands),
         out_specs=jax.tree.map(lambda _: VMEM, outs) if out_specs is None else out_specs,
         scratch_shapes=scratch,
-        compiler_params=pltpu.CompilerParams(vmem_limit_bytes=VMEM_LIMIT),
+        compiler_params=pltpu.CompilerParams(vmem_limit_bytes=limit),
         cost_estimate=pl.CostEstimate(flops=flops, bytes_accessed=flops // 128, transcendentals=0),
     )(*operands)
 
@@ -241,10 +303,10 @@
     return jax.ShapeDtypeStruct(shape, dtype)
 
 
-def exchange(array):
-    peers = math.prod(AXES[a] for a in PEERS)
-    blocks = array.reshape(peers, array.shape[0] // peers, array.shape[1])
-    blocks = lax.all_to_all(blocks, PEERS, split_axis=0, concat_axis=0, tiled=True)
+def exchange(array, peers):
+    count = math.prod(AXES[a] for a in peers)
+    blocks = array.reshape(count, array.shape[0] // count, array.shape[1])
+    blocks = lax.all_to_all(blocks, peers, split_axis=0, concat_axis=0, tiled=True)
     return blocks.reshape(array.shape)
 
 
@@ -257,37 +319,43 @@
     forward_scale = 1.0 / math.sqrt(cells * math.prod(AXES.values()))
     back_scale = 1.0 / math.sqrt(angles * kx_count * ky_count)
     columns = volume.reshape(cells, length)
-    forward = local_call(
-        functools.partial(forward_kernel, 1.0 / math.sqrt(length)),
-        shape_of(length, length),
-        (),
-        flops=2**10,
-    )
-    inverse = column_table(length, 1.0 / math.sqrt(planes))
-
-    sending = local_call(
-        transform_kernel,
-        shape_of(rows, LANES),
-        (columns, forward),
-    )
-    x_table, y_table = local_call(
-        tables_kernel,
-        (shape_of(PLANES, 32, 4 * LANES), shape_of(4 * LANES, 4 * LANES)),
+    forward = column_table(length, 1.0 / math.sqrt(length), OUT)
+    inverse = column_table(length, 1.0 / math.sqrt(planes), BACK)
+
+    sending, own, x_table, y_table = local_call(
+        start_kernel,
         (
-            x_frequency.transpose(1, 2, 0).reshape(angles * kx_count, planes),
-            y_frequency.transpose(1, 2, 0).reshape(angles * ky_count, planes),
-            sending,
+            shape_of(rows, LANES),
+            shape_of(32, LANES, dtype=F32),
+            shape_of(PLANES, 32, 4 * LANES),
+            shape_of(4 * LANES, 4 * LANES),
         ),
-        [pltpu.VMEM((planes, LANES), F32)],
-        [VMEM, VMEM, ANY],
-        flops=2**10,
-    )
-    x_table, y_table, sending = lax.optimization_barrier((x_table, y_table, sending))
-    received = exchange(sending)
+        (
+            pin(x_frequency.transpose(1, 2, 0).reshape(angles * kx_count, planes)),
+            pin(y_frequency.transpose(1, 2, 0).reshape(angles * ky_count, planes)),
+            pin(columns),
+            pin(jnp.asarray(forward)),
+            pin(measured[0]),
+            pin(weights[0]),
+        ),
+        [
+            pltpu.VMEM((angles * kx_count, planes), jnp.int32),
+            pltpu.VMEM((angles * ky_count, planes), jnp.int32),
+            pltpu.VMEM((cells, length), BF16),
+            pltpu.VMEM((length, length), BF16),
+            pltpu.VMEM(measured.shape[1:], F32),
+            pltpu.VMEM(weights.shape[1:], F32),
+            pltpu.VMEM((planes, LANES), F32),
+            pltpu.SemaphoreType.DMA((6,)),
+        ],
+        [HBM] * 6,
+        limit=START_LIMIT,
+    )
+    received = exchange(sending, OUT)
     points = local_call(
         functools.partial(predict_kernel, forward_scale),
         shape_of(PLANES, 32, LANES, dtype=F32),
-        (received, y_table, x_table, measured[0], weights[0]),
+        (received, y_table, x_table, own),
     )
     others = lax.ppermute(points, "c", SWAP)
     misfit, sending = local_call(
@@ -295,7 +363,7 @@
         (shape_of(angles * kx_count, LANES, dtype=F32), shape_of(rows, LANES)),
         (points, others, y_table, x_table),
     )
-    received = exchange(sending)
+    received = exchange(sending, BACK)
     updated = local_call(
         update_kernel,
         shape_of(cells, length),

time: 57.1 us -> 56.6 us (level)
  local copies, waits for them, and re-layouts: 1.21 us -> 0.01 us
  Pallas kernels: 3.98 us -> 4.64 us
    unnamed x12 -> x4, local copies, waits for them, and re-layouts: 1.21 us -> 0.01 us
    pallas_call x6 -> x4, Pallas kernels: 3.98 us -> 4.64 us  [local_call(): pl.pallas_call(kernel, out_shape=outs, in_specs=specs or [VMEM] * len(ope...]
where the time goes in v3:
time: 56.6 us; the launch traced here: 56.4 us
  blocking collectives  49.8 us (88%)
  Pallas kernels  4.64 us (8%)
  waiting for transfers between devices  1.19 us (2%)
  between operations  0.65 us (1%)
    all_to_all x2, blocking collectives, exchange(): lax.all_to_all(blocks, peers, split_axis=0, concat_axis=0, tiled=True)  49.8 us
    pallas_call x4, Pallas kernels, local_call(): pl.pallas_call(kernel, out_shape=outs, in_specs=specs or [VMEM] * len(ope...  4.64 us
    ppermute x1, waiting for transfers between devices, shards(): others = lax.ppermute(points, 'c', SWAP)  1.19 us
  transfers between devices with their start and end apart: 1, of which 1 were waited for; matrix products, arithmetic and copies ran while one was open for 0% of the time, Pallas kernels for 0%

profile of v3, /device:TPU:32, one launch (start us, length us, event | category | flops | bytes accessed | tf_op | source)
XLA Modules:
  0.0 56.4 jit_solution(674800569785559388)
XLA Ops:
  0.6 1.8 %shard_map.86 = (bf16[1024,128]{1,0:T(8,128)(2,1)S(1)}, f32[32,128]{1,0:T(8,128)S(1)}, bf16[2,32,512]{2,1,0:T(8,128)(2,1)S(1)}, bf16[512,512]{1,0:T(8,128)(2,1)S(1)}) custom-call(s32[16,256]{1,0:T(8,128)} %bitcast.23, s32[128,256]{1,0:T(8,128)} %bitcast.22, bf16[256,512]{1,0:T(8,128)(2,1)} %bitcast.17, bf16[512,512]{1,0:T(8,128)(2,1)} %constant.4.clone.forward_hbm, ...), custom_call_target="tpu_custom_call" | custom-call | flops 134217728 | bytes 1048576 | tf_op jit(solution)/shard_map/pallas_call | solution.py:291
  2.4 28.9 %all_to_all.10 = bf16[128,8,128]{2,1,0:T(8,128)(2,1)S(1)} all-to-all(bf16[128,8,128]{2,1,0:T(8,128)(2,1)S(1)} %bitcast.20), channel_id=1, replica_groups=mesh['y'=4,'zl'=4,'c'=2,'zh'=2,'x'=4] {'zl','y','x','zh'}, dimensions={0} | all-to-all | bytes 524288 | tf_op jit(solution)/shard_map/all_to_all | solution.py:309
  31.3 0.7 %shard_map.87.mine_ref = f32[2,32,128]{2,1,0:T(8,128)S(1)} custom-call(bf16[1024,128]{1,0:T(8,128)(2,1)S(1)} %bitcast.15, bf16[512,512]{1,0:T(8,128)(2,1)S(1)} %get-tuple-element.9.y_ref, bf16[2,32,512]{2,1,0:T(8,128)(2,1)S(1)} %get-tuple-element.10.x_ref, f32[32,128]{1,0:T(8,128)S(1)} %get-tuple-element.11.own_ref), custom_call_target="tpu_custom_call" | custom-call | flops 134217728 | bytes 1048576 | tf_op jit(solution)/shard_map/pallas_call | solution.py:291
  32.0 0.0 copy-start.1
  32.0 0.1 collective-permute-start
  32.1 1.2 %collective-permute-done.other_ref = f32[2,32,128]{2,1,0:T(8,128)S(1)} collective-permute-done((f32[2,32,128]{2,1,0:T(8,128)S(1)}, f32[2,32,128]{2,1,0:T(8,128)S(1)}, u32[]{:S(2)}, u32[]{:S(2)}) %collective-permute-start) | collective-permute-done | bytes 32800 | tf_op jit(solution)/shard_map/ppermute | solution.py:360
  33.3 1.1 %shard_map.88 = (f32[16,128]{1,0:T(8,128)}, bf16[1024,128]{1,0:T(8,128)(2,1)S(1)}) custom-call(f32[2,32,128]{2,1,0:T(8,128)S(1)} %shard_map.87.mine_ref, f32[2,32,128]{2,1,0:T(8,128)S(1)} %collective-permute-done.other_ref, bf16[512,512]{1,0:T(8,128)(2,1)S(1)} %get-tuple-element.9.y_ref, bf16[2,32,512]{2,1,0:T(8,128)(2,1)S(1)} %get-tuple-element.10.x_ref), custom_call_target="tpu_custom_call" | custom-call | flops 134217728 | bytes 1048576 | tf_op jit(solution)/shard_map/pallas_call | solution.py:291
  34.4 0.0 copy-start
  34.4 20.9 %all_to_all.11 = bf16[128,8,128]{2,1,0:T(8,128)(2,1)S(1)} all-to-all(bf16[128,8,128]{2,1,0:T(8,128)(2,1)S(1)} %bitcast.19), channel_id=1, replica_groups=mesh['y'=4,'zl'=4,'c'=2,'zh'=2,'x'=4] {'zl','y','x','zh'}, dimensions={0} | all-to-all | bytes 524288 | tf_op jit(solution)/shard_map/all_to_all | solution.py:309
  55.4 0.0 copy-done.1
  55.4 0.0 copy-done
  55.4 1.0 %shard_map.89 = bf16[256,512]{1,0:T(8,128)(2,1)} custom-call(bf16[1024,128]{1,0:T(8,128)(2,1)S(1)} %bitcast.16, bf16[256,512]{1,0:T(8,128)(2,1)S(1)} %bitcast.18, bf16[512,512]{1,0:T(8,128)(2,1)S(1)} %copy-done.1), custom_call_target="tpu_custom_call" | custom-call | flops 134217728 | bytes 1048576 | tf_op jit(solution)/shard_map/pallas_call | solution.py:291
Async XLA Ops:
  32.0 23.3 %copy-start.1 = (bf16[512,512]{1,0:T(8,128)(2,1)S(1)}, bf16[512,512]{1,0:T(8,128)(2,1)}, u32[]{:S(2)}) copy-start(bf16[512,512]{1,0:T(8,128)(2,1)} %constant.5.clone.table_ref) | copy-start | bytes 1572868
  32.0 1.3 %collective-permute-start = (f32[2,32,128]{2,1,0:T(8,128)S(1)}, f32[2,32,128]{2,1,0:T(8,128)S(1)}, u32[]{:S(2)}, u32[]{:S(2)}) collective-permute-start(f32[2,32,128]{2,1,0:T(8,128)S(1)} %shard_map.87.mine_ref), channel_id=1, source_target_pairs={{0,8},{8,0},{1,9},{9,1},{2,10},{10,2},{3,11},{11,3},{4,12},{12,4},... | collective-permute-start | bytes 98312 | tf_op jit(solution)/shard_map/ppermute | solution.py:360
  34.4 20.9 %copy-start = (bf16[8,32,512]{2,1,0:T(8,128)(2,1)S(1)}, bf16[8,32,512]{2,1,0:T(8,128)(2,1)}, u32[]{:S(2)}) copy-start(bf16[8,32,512]{2,1,0:T(8,128)(2,1)} %param.7) | copy-start | bytes 786436

commit v4 on v3

v4 whole, which is shorter than its diff:
```python
import functools
import math

import jax
import jax.numpy as jnp
import numpy as np
from jax import lax
from jax.experimental import pallas as pl
from jax.experimental.pallas import tpu as pltpu
from jax.sharding import Mesh
from jax.sharding import PartitionSpec as P

FINE = 4096
GRAIN = 32
LANES = 128
VMEM_LIMIT = 12 * 2**20
START_LIMIT = 12 * 2**20
F32 = jnp.float32
BF16 = jnp.bfloat16
AXES = {"y": 4, "zl": 4, "c": 2, "zh": 2, "x": 4}
SLAB = ("y", "zl", "c")
ROWS = ("zh", "x")
PEERS = ("zl", "y", "x", "zh")
PLANES = 2
SWAP = [(0, 1), (1, 0)]


def plane_of(**at):
    number = 0
    for axis in SLAB + ROWS:
        number = number * AXES[axis] + at[axis]
    return number


def column_table(length, scale):
    grid = np.arange(length // 2).reshape(4, 4, 2, 2, 2, 2)
    order = grid.transpose(1, 0, 4, 3, 5, 2).reshape(-1)
    depths = np.arange(length, dtype=np.int64)
    angles = (order[:, None] * depths[None, :] % length) * (2.0 * math.pi / length)
    matrix = np.stack([np.cos(angles), -np.sin(angles)], axis=1) * scale
    return matrix.reshape(length, length).astype(np.float32).astype(BF16)


def cosine_of_turns(turns):
    part = turns - jnp.floor(turns + 0.5)
    angle = (0.25 - jnp.abs(part)) * (2.0 * math.pi)
    square = angle * angle
    series = -1.0 / 39916800.0
    for term in (362880.0, -5040.0, 120.0, -6.0):
        series = series * square + 1.0 / term
    return angle + angle * square * series


def phases(turns):
    return cosine_of_turns(turns), cosine_of_turns(turns + 0.25)


def dot(left, right, left_dim, right_dim):
    dims = (((left_dim,), (right_dim,)), ((), ()))
    return lax.dot_general(left, right, dims, preferred_element_type=F32)


def iota(shape, axis):
    return lax.broadcasted_iota(jnp.int32, shape, axis)


def exchange_grains(blocks):
    lane = iota(blocks[0].shape, 1)
    low = lane < 2 * GRAIN
    even = (lane & GRAIN) == 0
    first = [None] * 4
    for i in (0, 1):
        a, b = blocks[i], blocks[i + 2]
        first[i] = jnp.where(low, a, pltpu.roll(b, 2 * GRAIN, 1))
        first[i + 2] = jnp.where(low, pltpu.roll(a, 2 * GRAIN, 1), b)
    last = [None] * 4
    for i in (0, 2):
        a, b = first[i], first[i + 1]
        last[i] = jnp.where(even, a, pltpu.roll(b, GRAIN, 1))
        last[i + 1] = jnp.where(even, pltpu.roll(a, 3 * GRAIN, 1), b)
    return last


def start_kernel(
    x_hbm,
    y_hbm,
    columns_hbm,
    forward_hbm,
    measured_hbm,
    weights_hbm,
    out_ref,
    own_ref,
    x_table_ref,
    y_table_ref,
    x_own,
    y_all,
    columns,
    forward,
    measured,
    weights,
    turned,
    sems,
):
    pairs = (
        (x_hbm, x_own),
        (y_hbm, y_all),
        (columns_hbm, columns),
        (forward_hbm, forward),
        (measured_hbm, measured),
        (weights_hbm, weights),
    )
    loads = [pltpu.make_async_copy(a, b, sems.at[i]) for i, (a, b) in enumerate(pairs)]
    for load in loads:
        load.start()
    at = {a: lax.axis_index(a) for a in SLAB + ROWS}
    lane = iota((16, 2 * LANES), 1)
    x_at = (lane >> 3 & 1) * 32 + (lane >> 4 & 3) * 8 + (lane >> 2 & 1) * 4 + (lane >> 6)
    x_at = x_at.astype(F32) * (1.0 / FINE)
    x_shift = (lane & 1).astype(F32) * 0.75
    team = lane >> 1 & 1
    y_in = iota((32, LANES), 0).astype(F32)
    y_block = (iota((16, LANES), 0) * 64 + at["c"] * 32).astype(F32)
    plane = [plane_of(**{**at, "c": p}) for p in range(PLANES)]
    for load in loads[:2]:
        load.wait()
    turned[...] = y_all[...].astype(F32).T
    x_all = x_own[...].astype(F32)
    lane_plane = iota(x_all.shape, 1)
    kx = [
        jnp.sum(jnp.where(lane_plane == k, x_all, 0.0), axis=1, keepdims=True) + FINE / 2.0
        for k in plane
    ]
    real, imag = phases(jnp.where(team == 0, kx[0], kx[1]) * x_at + x_shift)
    for p in range(PLANES):
        own_real = jnp.where(team == p, real, 0.0)
        own_imag = jnp.where(team == p, imag, 0.0)
        near, far = pl.ds(32 * p, 16), pl.ds(32 * p + 16, 16)
        x_table_ref[near, : 2 * LANES] = own_real.astype(BF16)
        x_table_ref[near, 2 * LANES :] = (-own_imag).astype(BF16)
        x_table_ref[far, : 2 * LANES] = own_imag.astype(BF16)
        x_table_ref[far, 2 * LANES :] = own_real.astype(BF16)
        ky = (turned[pl.ds(plane[p], 1), :] + FINE / 2.0) * (1.0 / FINE)
        fine = phases(ky * y_in)
        coarse = phases(ky * y_block)
        for b in range(16):
            real_b, imag_b = coarse[0][b : b + 1], coarse[1][b : b + 1]
            rows = pl.ds(b * 32, 32)
            near, far = pl.ds(p * LANES, LANES), pl.ds((PLANES + p) * LANES, LANES)
            y_table_ref[rows, near] = (real_b * fine[0] - imag_b * fine[1]).astype(BF16)
            y_table_ref[rows, far] = (real_b * fine[1] + imag_b * fine[0]).astype(BF16)
    for load in loads[2:]:
        load.wait()
    own_ref[:16] = measured[...]
    own_ref[16:, LANES // 2 :] = jnp.zeros((16, LANES // 2), F32)
    own_ref[16:, : LANES // 2] = weights[...]
    spectrum = dot(forward[...], columns[...], 1, 1).astype(BF16)
    near = spectrum[:, :LANES].reshape(-1, 16, LANES)
    far = spectrum[:, LANES:].reshape(-1, 16, LANES)
    even = (iota(near.shape, 1) & 4) == 0
    first = jnp.where(even, near, pltpu.roll(far, 4, 1))
    second = jnp.where(even, pltpu.roll(near, 12, 1), far)
    out_ref[...] = jnp.stack([first, second], axis=1).reshape(out_ref.shape)


def predict_kernel(scale, planes_ref, y_ref, x_ref, own_ref, out_ref):
    quarter = planes_ref.shape[0] // 4
    blocks = [planes_ref[pl.ds(g * quarter, quarter), :] for g in range(4)]
    blocks = exchange_grains(blocks)
    rows = quarter // 4
    left = [
        jnp.concatenate([b[i * rows : i * rows + rows] for b in blocks], axis=0)
        for i in range(4)
    ]
    inner = dot(jnp.concatenate(left, axis=1), y_ref[...], 1, 0).astype(BF16)
    inner = jnp.concatenate([inner[:, : 2 * LANES], inner[:, 2 * LANES :]], axis=0)
    both = dot(x_ref[...], inner, 1, 0)
    first = iota((8, LANES), 1) < LANES // 2
    for p in range(PLANES):
        points = both[32 * p : 32 * p + 32, LANES * p : LANES * p + LANES] * scale
        real, imag = points[:16], points[16:]
        out_ref[p, :8] = jnp.where(first, real[:8], pltpu.roll(imag[:8], 64, 1))
        out_ref[p, 8:16] = jnp.where(first, pltpu.roll(real[8:], 64, 1), imag[8:])
        out_ref[p, 16:] = jnp.zeros((16, LANES), F32)
    own = lax.axis_index("c")
    out_ref[own, :16] = out_ref[own, :16] - own_ref[:16]
    out_ref[own, 16:] = own_ref[16:]


def spread_kernel(scale, mine_ref, other_ref, y_ref, x_ref, misfit_ref, out_ref):
    first = iota((8, LANES), 1) < LANES // 2
    zero = jnp.zeros((8, LANES), F32)

    def both(weight):
        return jnp.where(first, weight, pltpu.roll(weight, 64, 1))

    def misfit_of(total):
        return total[:8] * both(total[16:24]), total[8:16] * both(total[24:])

    lanes = []
    for p in range(PLANES):
        near, far = misfit_of(mine_ref[p] + other_ref[p])
        near, far = near * scale, far * scale
        spread = [
            jnp.where(first, near, zero),
            jnp.where(first, zero, pltpu.roll(far, 64, 1)),
            jnp.where(first, pltpu.roll(near, 64, 1), zero),
            jnp.where(first, zero, far),
        ]
        lanes.append(jnp.concatenate([zero] * 4 * p + spread + [zero] * 4 * (1 - p), axis=0))
    inner = dot(x_ref[...], jnp.concatenate(lanes, axis=1).astype(BF16), 0, 0).astype(BF16)
    inner = jnp.concatenate([inner[: 2 * LANES], inner[2 * LANES :]], axis=1)
    planes = dot(inner, y_ref[...], 1, 1).astype(BF16)
    rows = planes.shape[0] // 4
    for i in range(4):
        lanes = slice(i * LANES, i * LANES + LANES)
        blocks = [planes[q * rows : q * rows + rows, lanes] for q in range(4)]
        blocks = exchange_grains(blocks)
        for g in range(4):
            out_ref[pl.ds((4 * g + i) * rows, rows), :] = blocks[g]
    own = lax.axis_index("c")
    near, far = misfit_of(mine_ref[own] + other_ref[own])
    misfit_ref[:8], misfit_ref[8:] = near, far


def update_kernel(planes_ref, columns_ref, table_ref, out_hbm, staged, sems):
    planes = planes_ref[...].reshape(-1, 2, 16, LANES)
    first, second = planes[:, 0], planes[:, 1]
    even = (iota(first.shape, 1) & 4) == 0
    near = jnp.where(even, first, pltpu.roll(second, 4, 1)).reshape(-1, LANES)
    far = jnp.where(even, pltpu.roll(first, 12, 1), second).reshape(-1, LANES)
    table = table_ref[...]
    stores = []
    for i, back in enumerate((near, far)):
        part = pl.ds(i * LANES, LANES)
        correction = dot(back, table, 0, 0)
        staged[part, :] = (columns_ref[part, :].astype(F32) - 0.5 * correction).astype(BF16)
        stores.append(pltpu.make_async_copy(staged.at[part], out_hbm.at[part], sems.at[i]))
        stores[-1].start()
    for store in stores:
        store.wait()


VMEM = pl.BlockSpec(memory_space=pltpu.VMEM)
ANY = pl.BlockSpec(memory_space=pl.ANY)
HBM = pl.BlockSpec(memory_space=pltpu.HBM)


def pin(array):
    return pltpu.with_memory_space_constraint(array, pltpu.HBM)


def local_call(kernel, outs, operands, scratch=(), specs=None, out_specs=None, flops=2**27, limit=VMEM_LIMIT):
    return pl.pallas_call(
        kernel,
        out_shape=outs,
        in_specs=specs or [VMEM] * len(operands),
        out_specs=jax.tree.map(lambda _: VMEM, outs) if out_specs is None else out_specs,
        scratch_shapes=scratch,
        compiler_params=pltpu.CompilerParams(vmem_limit_bytes=limit),
        cost_estimate=pl.CostEstimate(flops=flops, bytes_accessed=flops // 128, transcendentals=0),
    )(*operands)


def shape_of(*shape, dtype=BF16):
    return jax.ShapeDtypeStruct(shape, dtype)


def exchange(array):
    count = math.prod(AXES[a] for a in PEERS)
    blocks = array.reshape(count, array.shape[0] // count, array.shape[1])
    blocks = lax.all_to_all(blocks, PEERS, split_axis=0, concat_axis=0, tiled=True)
    return blocks.reshape(array.shape)


def shards(volume, x_frequency, y_frequency, measured, weights):
    x_local, y_local, length = volume.shape
    cells = x_local * y_local
    rows = cells * length // LANES
    planes, angles, kx_count = x_frequency.shape
    ky_count = y_frequency.shape[2]
    forward_scale = 1.0 / math.sqrt(cells * math.prod(AXES.values()))
    back_scale = 1.0 / math.sqrt(angles * kx_count * ky_count)
    columns = volume.reshape(cells, length)
    forward = column_table(length, 1.0 / math.sqrt(length))
    inverse = column_table(length, 1.0 / math.sqrt(planes))

    sending, own, x_table, y_table = local_call(
        start_kernel,
        (
            shape_of(rows, LANES),
            shape_of(32, LANES, dtype=F32),
            shape_of(PLANES * 32, 4 * LANES),
            shape_of(4 * LANES, 4 * LANES),
        ),
        (
            pin(x_frequency.transpose(1, 2, 0).reshape(angles * kx_count, planes)),
            pin(y_frequency.transpose(1, 2, 0).reshape(angles * ky_count, planes)),
            pin(columns),
            pin(jnp.asarray(forward)),
            pin(measured[0]),
            pin(weights[0]),
        ),
        [
            pltpu.VMEM((angles * kx_count, planes), jnp.int32),
            pltpu.VMEM((angles * ky_count, planes), jnp.int32),
            pltpu.VMEM((cells, length), BF16),
            pltpu.VMEM((length, length), BF16),
            pltpu.VMEM(measured.shape[1:], F32),
            pltpu.VMEM(weights.shape[1:], F32),
            pltpu.VMEM((planes, LANES), F32),
            pltpu.SemaphoreType.DMA((6,)),
        ],
        [HBM] * 6,
        limit=START_LIMIT,
    )
    received = exchange(sending)
    points = local_call(
        functools.partial(predict_kernel, forward_scale),
        shape_of(PLANES, 32, LANES, dtype=F32),
        (received, y_table, x_table, own),
    )
    others = lax.ppermute(points, "c", SWAP)
    misfit, sending = local_call(
        functools.partial(spread_kernel, back_scale),
        (shape_of(angles * kx_count, LANES, dtype=F32), shape_of(rows, LANES)),
        (points, others, y_table, x_table),
    )
    received = exchange(sending)
    updated = local_call(
        update_kernel,
        shape_of(cells, length),
        (received, columns, inverse),
        [pltpu.VMEM((cells, length), BF16), pltpu.SemaphoreType.DMA((2,))],
        out_specs=ANY,
    )
    return (updated.reshape(volume.shape), misfit.reshape(measured.shape))


def solution(mesh):
    fine = Mesh(mesh.devices.reshape(tuple(AXES.values())), tuple(AXES))
    placed = (
        P(ROWS, SLAB, None),
        P(),
        P(),
        P(SLAB + ROWS, None, None),
        P(SLAB + ROWS, None, None),
    )
    return jax.shard_map(
        shards,
        mesh=fine,
        in_specs=placed,
        out_specs=(P(ROWS, SLAB, None), P(SLAB + ROWS, None, None)),
        check_vma=False,
    )
```

time: 56.6 us -> 56.4 us (level)
  no operation moved by 1% of the time
where the time goes in v4:
time: 56.4 us; the launch traced here: 56.2 us
  blocking collectives  49.8 us (88%)
  Pallas kernels  4.43 us (8%)
  waiting for transfers between devices  1.19 us (2%)
  between operations  0.65 us (1%)
    all_to_all x2, blocking collectives, exchange(): lax.all_to_all(blocks, PEERS, split_axis=0, concat_axis=0, tiled=True)  49.8 us
    pallas_call x4, Pallas kernels, local_call(): pl.pallas_call(kernel, out_shape=outs, in_specs=specs or [VMEM] * len(ope...  4.43 us
    ppermute x1, waiting for transfers between devices, shards(): others = lax.ppermute(points, 'c', SWAP)  1.19 us
  transfers between devices with their start and end apart: 1, of which 1 were waited for; matrix products, arithmetic and copies ran while one was open for 0% of the time, Pallas kernels for 0%

profile of v4, /device:TPU:32, one launch (start us, length us, event | category | flops | bytes accessed | tf_op | source)
XLA Modules:
  0.0 56.2 jit_solution(12230453736717289807)
XLA Ops:
  0.6 1.7 %shard_map.86 = (bf16[1024,128]{1,0:T(8,128)(2,1)S(1)}, f32[32,128]{1,0:T(8,128)S(1)}, bf16[64,512]{1,0:T(8,128)(2,1)S(1)}, bf16[512,512]{1,0:T(8,128)(2,1)S(1)}) custom-call(s32[16,256]{1,0:T(8,128)} %bitcast.23, s32[128,256]{1,0:T(8,128)} %bitcast.22, bf16[256,512]{1,0:T(8,128)(2,1)} %bitcast.17, bf16[512,512]{1,0:T(8,128)(2,1)} %constant.4.clone.forward_hbm, ...), custom_call_target="tpu_custom_call" | custom-call | flops 134217728 | bytes 1048576 | tf_op jit(solution)/shard_map/pallas_call | solution.py:253
  2.3 28.9 %all_to_all.10 = bf16[128,8,128]{2,1,0:T(8,128)(2,1)S(1)} all-to-all(bf16[128,8,128]{2,1,0:T(8,128)(2,1)S(1)} %bitcast.20), channel_id=1, replica_groups=mesh['y'=4,'zl'=4,'c'=2,'zh'=2,'x'=4] {'zl','y','x','zh'}, dimensions={0} | all-to-all | bytes 524288 | tf_op jit(solution)/shard_map/all_to_all | solution.py:271
  31.2 0.7 %shard_map.87.mine_ref = f32[2,32,128]{2,1,0:T(8,128)S(1)} custom-call(bf16[1024,128]{1,0:T(8,128)(2,1)S(1)} %bitcast.15, bf16[512,512]{1,0:T(8,128)(2,1)S(1)} %get-tuple-element.9.y_ref, bf16[64,512]{1,0:T(8,128)(2,1)S(1)} %get-tuple-element.10.x_ref, f32[32,128]{1,0:T(8,128)S(1)} %get-tuple-element.11.own_ref), custom_call_target="tpu_custom_call" | custom-call | flops 134217728 | bytes 1048576 | tf_op jit(solution)/shard_map/pallas_call | solution.py:253
  31.9 0.0 copy-start.1
  31.9 0.1 collective-permute-start
  32.0 1.2 %collective-permute-done.other_ref = f32[2,32,128]{2,1,0:T(8,128)S(1)} collective-permute-done((f32[2,32,128]{2,1,0:T(8,128)S(1)}, f32[2,32,128]{2,1,0:T(8,128)S(1)}, u32[]{:S(2)}, u32[]{:S(2)}) %collective-permute-start) | collective-permute-done | bytes 32800 | tf_op jit(solution)/shard_map/ppermute | solution.py:322
  33.2 1.0 %shard_map.88 = (f32[16,128]{1,0:T(8,128)}, bf16[1024,128]{1,0:T(8,128)(2,1)S(1)}) custom-call(f32[2,32,128]{2,1,0:T(8,128)S(1)} %shard_map.87.mine_ref, f32[2,32,128]{2,1,0:T(8,128)S(1)} %collective-permute-done.other_ref, bf16[512,512]{1,0:T(8,128)(2,1)S(1)} %get-tuple-element.9.y_ref, bf16[64,512]{1,0:T(8,128)(2,1)S(1)} %get-tuple-element.10.x_ref), custom_call_target="tpu_custom_call" | custom-call | flops 134217728 | bytes 1048576 | tf_op jit(solution)/shard_map/pallas_call | solution.py:253
  34.3 0.0 copy-start
  34.3 20.9 %all_to_all.11 = bf16[128,8,128]{2,1,0:T(8,128)(2,1)S(1)} all-to-all(bf16[128,8,128]{2,1,0:T(8,128)(2,1)S(1)} %bitcast.19), channel_id=1, replica_groups=mesh['y'=4,'zl'=4,'c'=2,'zh'=2,'x'=4] {'zl','y','x','zh'}, dimensions={0} | all-to-all | bytes 524288 | tf_op jit(solution)/shard_map/all_to_all | solution.py:271
  55.2 0.0 copy-done.1
  55.2 0.0 copy-done
  55.2 1.0 %shard_map.89 = bf16[256,512]{1,0:T(8,128)(2,1)} custom-call(bf16[1024,128]{1,0:T(8,128)(2,1)S(1)} %bitcast.16, bf16[256,512]{1,0:T(8,128)(2,1)S(1)} %bitcast.18, bf16[512,512]{1,0:T(8,128)(2,1)S(1)} %copy-done.1), custom_call_target="tpu_custom_call" | custom-call | flops 134217728 | bytes 1048576 | tf_op jit(solution)/shard_map/pallas_call | solution.py:253
Async XLA Ops:
  31.9 23.3 %copy-start.1 = (bf16[512,512]{1,0:T(8,128)(2,1)S(1)}, bf16[512,512]{1,0:T(8,128)(2,1)}, u32[]{:S(2)}) copy-start(bf16[512,512]{1,0:T(8,128)(2,1)} %constant.5.clone.table_ref) | copy-start | bytes 1572868
  31.9 1.3 %collective-permute-start = (f32[2,32,128]{2,1,0:T(8,128)S(1)}, f32[2,32,128]{2,1,0:T(8,128)S(1)}, u32[]{:S(2)}, u32[]{:S(2)}) collective-permute-start(f32[2,32,128]{2,1,0:T(8,128)S(1)} %shard_map.87.mine_ref), channel_id=1, source_target_pairs={{0,8},{8,0},{1,9},{9,1},{2,10},{10,2},{3,11},{11,3},{4,12},{12,4},... | collective-permute-start | bytes 98312 | tf_op jit(solution)/shard_map/ppermute | solution.py:322
  34.3 20.9 %copy-start = (bf16[8,32,512]{2,1,0:T(8,128)(2,1)S(1)}, bf16[8,32,512]{2,1,0:T(8,128)(2,1)}, u32[]{:S(2)}) copy-start(bf16[8,32,512]{2,1,0:T(8,128)(2,1)} %param.7) | copy-start | bytes 786436

commit v5 on v4

v5 whole, which is shorter than its diff:
```python
import functools
import math

import jax
import jax.numpy as jnp
import numpy as np
from jax import lax
from jax.experimental import pallas as pl
from jax.experimental.pallas import tpu as pltpu
from jax.sharding import Mesh
from jax.sharding import PartitionSpec as P

FINE = 4096
LANES = 128
VMEM_LIMIT = 12 * 2**20
F32 = jnp.float32
BF16 = jnp.bfloat16
AXES = {"yh": 2, "yl": 2, "zl": 4, "c": 2, "zh": 2, "x": 4}
SLAB = ("yh", "yl", "zl", "c")
ROWS = ("zh", "x")
PEERS = ("zl", "yl", "zh", "x")
TEAM = ("yh", "c")
PLANES = 4
SWAP = [(0, 1), (1, 0)]


def plane_of(at):
    number = 0
    for axis in SLAB + ROWS:
        number = number * AXES[axis] + at[axis]
    return number


def column_table(length, scale):
    grid = np.arange(length // 2).reshape([AXES[a] for a in SLAB + ROWS])
    order = grid.transpose([(SLAB + ROWS).index(a) for a in PEERS + TEAM]).reshape(-1)
    depths = np.arange(length, dtype=np.int64)
    angles = (order[:, None] * depths[None, :] % length) * (2.0 * math.pi / length)
    matrix = np.stack([np.cos(angles), -np.sin(angles)], axis=1) * scale
    return matrix.reshape(length, length).astype(np.float32).astype(BF16)


def cosine_of_turns(turns):
    part = turns - jnp.floor(turns + 0.5)
    angle = (0.25 - jnp.abs(part)) * (2.0 * math.pi)
    square = angle * angle
    series = -1.0 / 39916800.0
    for term in (362880.0, -5040.0, 120.0, -6.0):
        series = series * square + 1.0 / term
    return angle + angle * square * series


def phases(turns):
    return cosine_of_turns(turns), cosine_of_turns(turns + 0.25)


def product(left, right):
    return (
        left[0] * right[0] - left[1] * right[1],
        left[0] * right[1] + left[1] * right[0],
    )


def dot(left, right, left_dim, right_dim):
    dims = (((left_dim,), (right_dim,)), ((), ()))
    return lax.dot_general(left, right, dims, preferred_element_type=F32)


def iota(shape, axis):
    return lax.broadcasted_iota(jnp.int32, shape, axis)


def exchange_grains(blocks, axis, grain):
    size = blocks[0].shape[axis]
    place = iota(blocks[0].shape, axis) & (4 * grain - 1)
    low = place < 2 * grain
    even = (place & grain) == 0
    first = [None] * 4
    for i in (0, 1):
        a, b = blocks[i], blocks[i + 2]
        first[i] = jnp.where(low, a, pltpu.roll(b, 2 * grain, axis))
        first[i + 2] = jnp.where(low, pltpu.roll(a, size - 2 * grain, axis), b)
    last = [None] * 4
    for i in (0, 2):
        a, b = first[i], first[i + 1]
        last[i] = jnp.where(even, a, pltpu.roll(b, grain, axis))
        last[i + 1] = jnp.where(even, pltpu.roll(a, size - grain, axis), b)
    return last


def start_kernel(
    x_hbm,
    y_hbm,
    columns_hbm,
    forward_hbm,
    measured_hbm,
    weights_hbm,
    out_ref,
    own_ref,
    x_table_ref,
    y_table_ref,
    x_all,
    y_all,
    columns,
    forward,
    measured,
    weights,
    turned,
    sems,
):
    pairs = (
        (x_hbm, x_all),
        (y_hbm, y_all),
        (columns_hbm, columns),
        (forward_hbm, forward),
        (measured_hbm, measured),
        (weights_hbm, weights),
    )
    loads = [pltpu.make_async_copy(a, b, sems.at[i]) for i, (a, b) in enumerate(pairs)]
    for load in loads:
        load.start()
    at = {a: lax.axis_index(a) for a in SLAB + ROWS}
    lane = iota((16, LANES), 1)
    x_at = (lane >> 4 & 1) * 32 + (lane >> 1 & 3) * 8 + (lane >> 3 & 1) * 4 + (lane >> 5)
    x_at = x_at.astype(F32) * (1.0 / FINE)
    x_shift = (lane & 1).astype(F32) * 0.75
    y_in = iota((32, LANES), 0).astype(F32)
    block = iota((8, LANES), 0)
    y_block = (block * 64 + at["yh"] * 512 + at["c"] * 32).astype(F32)
    plane = [plane_of({**at, "yh": p >> 1, "c": p & 1}) for p in range(PLANES)]
    for load in loads[:2]:
        load.wait()
    turned[...] = y_all[...].astype(F32).T
    x_own = x_all[...].astype(F32)
    lane_plane = iota(x_own.shape, 1)
    for p in range(PLANES):
        ky = (turned[pl.ds(plane[p], 1), :] + FINE / 2.0) * (1.0 / FINE)
        fine = phases(ky * y_in)
        coarse = phases(ky * y_block)
        for b in range(8):
            real, imag = product((coarse[0][b : b + 1], coarse[1][b : b + 1]), fine)
            y_table_ref[p, pl.ds(b * 32, 32), :LANES] = real.astype(BF16)
            y_table_ref[p, pl.ds(b * 32, 32), LANES:] = imag.astype(BF16)
        kx = jnp.sum(jnp.where(lane_plane == plane[p], x_own, 0.0), axis=1, keepdims=True)
        real, imag = phases((kx + FINE / 2.0) * x_at + x_shift)
        real, imag, back = real.astype(BF16), imag.astype(BF16), (-imag).astype(BF16)
        x_table_ref[pl.ds(32 * p, 16), :LANES] = real
        x_table_ref[pl.ds(32 * p, 16), LANES:] = back
        x_table_ref[pl.ds(32 * p + 16, 16), :LANES] = imag
        x_table_ref[pl.ds(32 * p + 16, 16), LANES:] = real
    for load in loads[2:]:
        load.wait()
    own_ref[:16] = measured[...]
    own_ref[16:, : LANES // 2] = weights[:8]
    own_ref[16:, LANES // 2 :] = weights[8:]
    spectrum = dot(forward[...], columns[...], 1, 1)
    near = spectrum[:, :LANES].reshape(-1, 8, LANES)
    far = spectrum[:, LANES:].reshape(-1, 8, LANES)
    out_ref[...] = jnp.concatenate([near, far], axis=1).reshape(out_ref.shape).astype(BF16)


def own_plane():
    return lax.axis_index("yh") * 2 + lax.axis_index("c")


def predict_kernel(scale, planes_ref, y_ref, x_ref, own_ref, out_ref):
    quarter = planes_ref.shape[0] // 4
    blocks = [planes_ref[pl.ds(g * quarter, quarter), :] for g in range(4)]
    blocks = exchange_grains(blocks, 1, 32)
    left = [[[], []] for _ in range(PLANES)]
    for q in range(4):
        rows = blocks[q].reshape(2, 2, 4, 16, LANES)
        for i in range(2):
            parts = exchange_grains([rows[i, :, x] for x in range(4)], 1, 2)
            for p in range(PLANES):
                left[p][i].append(parts[p].reshape(-1, LANES))
    near, far = [], []
    for p in range(PLANES):
        side = jnp.concatenate([jnp.concatenate(half, axis=0) for half in left[p]], axis=1)
        inner = dot(side, y_ref[p], 1, 0).astype(BF16)
        near.append(inner[:, :LANES])
        far.append(inner[:, LANES:])
    inner = jnp.concatenate(
        [jnp.concatenate(near, axis=1), jnp.concatenate(far, axis=1)], axis=0
    )
    everything = dot(x_ref[...], inner, 1, 0)
    first = iota((8, LANES), 1) < LANES // 2
    for p in range(PLANES):
        points = everything[32 * p : 32 * p + 32, LANES * p : LANES * p + LANES] * scale
        real, imag = points[:16], points[16:]
        out_ref[p, :8] = jnp.where(first, real[:8], pltpu.roll(imag[:8], 64, 1))
        out_ref[p, 8:16] = jnp.where(first, pltpu.roll(real[8:], 64, 1), imag[8:])
        out_ref[p, 16:] = jnp.zeros((8, LANES), F32)
    own = own_plane()
    out_ref[own, :16] = out_ref[own, :16] - own_ref[:16]
    out_ref[own, 16:] = own_ref[16:]


def spread_kernel(scale, sum_ref, other_ref, y_ref, x_ref, misfit_ref, out_ref):
    first = iota((8, LANES), 1) < LANES // 2

    def misfit_of(total):
        near, far, weight = total[:8], total[8:16], total[16:]
        crossed = pltpu.roll(weight, 64, 1)
        return (
            near * jnp.where(first, weight, crossed),
            far * jnp.where(first, crossed, weight),
        )

    zero = jnp.zeros((8, LANES), F32)
    lanes = []
    for p in range(PLANES):
        near, far = misfit_of(sum_ref[p] + other_ref[p].astype(F32))
        near, far = near * scale, far * scale
        spread = [
            jnp.where(first, near, zero),
            jnp.where(first, zero, pltpu.roll(far, 64, 1)),
            jnp.where(first, pltpu.roll(near, 64, 1), zero),
            jnp.where(first, zero, far),
        ]
        before, after = [zero] * 4 * p, [zero] * 4 * (PLANES - 1 - p)
        lanes.append(jnp.concatenate(before + spread + after, axis=0))
    everything = dot(x_ref[...], jnp.concatenate(lanes, axis=1).astype(BF16), 0, 0).astype(BF16)
    planes = []
    for p in range(PLANES):
        inner = everything[:, LANES * p : LANES * p + LANES]
        inner = jnp.concatenate([inner[:LANES], inner[LANES:]], axis=1)
        plane = dot(inner, y_ref[p], 1, 1).astype(BF16)
        planes.append(plane.reshape(4, 2, 16, 2 * LANES))
    blocks = []
    for q in range(4):
        rows = []
        for i in range(2):
            part = slice(i * LANES, i * LANES + LANES)
            parts = exchange_grains([planes[p][q, :, :, part] for p in range(PLANES)], 1, 2)
            rows.append(jnp.stack(parts, axis=1).reshape(-1, LANES))
        blocks.append(jnp.concatenate(rows, axis=0))
    blocks = exchange_grains(blocks, 1, 32)
    quarter = out_ref.shape[0] // 4
    for g in range(4):
        out_ref[pl.ds(g * quarter, quarter), :] = blocks[g]
    own = own_plane()
    near, far = misfit_of(sum_ref[own] + other_ref[own].astype(F32))
    misfit_ref[:8], misfit_ref[8:] = near, far


def update_kernel(planes_ref, columns_ref, table_ref, out_hbm, staged, sems):
    planes = planes_ref[...].astype(F32).reshape(-1, 2, 8, LANES)
    table = table_ref[...]
    stores = []
    for i in range(2):
        part = pl.ds(i * LANES, LANES)
        correction = dot(planes[:, i].reshape(-1, LANES).astype(BF16), table, 0, 0)
        staged[part, :] = (columns_ref[part, :].astype(F32) - 0.5 * correction).astype(BF16)
        stores.append(pltpu.make_async_copy(staged.at[part], out_hbm.at[part], sems.at[i]))
        stores[-1].start()
    for store in stores:
        store.wait()


VMEM = pl.BlockSpec(memory_space=pltpu.VMEM)
HBM = pl.BlockSpec(memory_space=pltpu.HBM)
ANY = pl.BlockSpec(memory_space=pl.ANY)


def pin(array):
    return pltpu.with_memory_space_constraint(array, pltpu.HBM)


def local_call(kernel, outs, operands, scratch=(), specs=None, out_specs=None):
    return pl.pallas_call(
        kernel,
        out_shape=outs,
        in_specs=specs or [VMEM] * len(operands),
        out_specs=jax.tree.map(lambda _: VMEM, outs) if out_specs is None else out_specs,
        scratch_shapes=scratch,
        compiler_params=pltpu.CompilerParams(vmem_limit_bytes=VMEM_LIMIT),
        cost_estimate=pl.CostEstimate(flops=2**27, bytes_accessed=2**20, transcendentals=0),
    )(*operands)


def shape_of(*shape, dtype=BF16):
    return jax.ShapeDtypeStruct(shape, dtype)


def exchange(array):
    count = math.prod(AXES[a] for a in PEERS)
    blocks = array.reshape(count, array.shape[0] // count, array.shape[1])
    blocks = lax.all_to_all(blocks, PEERS, split_axis=0, concat_axis=0, tiled=True)
    return blocks.reshape(array.shape)


def shards(volume, x_frequency, y_frequency, measured, weights):
    x_local, y_local, length = volume.shape
    cells = x_local * y_local
    rows = cells * length // LANES
    planes, angles, kx_count = x_frequency.shape
    ky_count = y_frequency.shape[2]
    forward_scale = 1.0 / math.sqrt(cells * math.prod(AXES.values()))
    back_scale = 1.0 / math.sqrt(angles * kx_count * ky_count)
    columns = volume.reshape(cells, length)
    forward = column_table(length, 1.0 / math.sqrt(length))
    inverse = column_table(length, 1.0 / math.sqrt(planes))

    sending, own, x_table, y_table = local_call(
        start_kernel,
        (
            shape_of(rows, LANES),
            shape_of(24, LANES, dtype=F32),
            shape_of(PLANES * 32, 2 * LANES),
            shape_of(PLANES, 2 * LANES, 2 * LANES),
        ),
        (
            pin(x_frequency.transpose(1, 2, 0).reshape(angles * kx_count, planes)),
            pin(y_frequency.transpose(1, 2, 0).reshape(angles * ky_count, planes)),
            pin(columns),
            pin(jnp.asarray(forward)),
            pin(measured[0]),
            pin(weights[0]),
        ),
        [
            pltpu.VMEM((angles * kx_count, planes), jnp.int32),
            pltpu.VMEM((angles * ky_count, planes), jnp.int32),
            pltpu.VMEM((cells, length), BF16),
            pltpu.VMEM((length, length), BF16),
            pltpu.VMEM(measured.shape[1:], F32),
            pltpu.VMEM(weights.shape[1:], F32),
            pltpu.VMEM((planes, LANES), F32),
            pltpu.SemaphoreType.DMA((6,)),
        ],
        [HBM] * 6,
    )
    received = exchange(sending)
    total = local_call(
        functools.partial(predict_kernel, forward_scale),
        shape_of(PLANES, 24, LANES, dtype=F32),
        (received, y_table, x_table, own),
    )
    total = total + lax.ppermute(total, "c", SWAP)
    other = lax.ppermute(total.astype(BF16), "yh", SWAP)
    misfit, sending = local_call(
        functools.partial(spread_kernel, back_scale),
        (shape_of(angles * kx_count, LANES, dtype=F32), shape_of(rows, LANES)),
        (total, other, y_table, x_table),
    )
    received = exchange(sending)
    updated = local_call(
        update_kernel,
        shape_of(cells, length),
        (received, columns, inverse),
        [pltpu.VMEM((cells, length), BF16), pltpu.SemaphoreType.DMA((2,))],
        out_specs=ANY,
    )
    return (updated.reshape(volume.shape), misfit.reshape(measured.shape))


def solution(mesh):
    fine = Mesh(mesh.devices.reshape(tuple(AXES.values())), tuple(AXES))
    placed = (
        P(ROWS, SLAB, None),
        P(),
        P(),
        P(SLAB + ROWS, None, None),
        P(SLAB + ROWS, None, None),
    )
    return jax.shard_map(
        shards,
        mesh=fine,
        in_specs=placed,
        out_specs=(P(ROWS, SLAB, None), P(SLAB + ROWS, None, None)),
        check_vma=False,
    )
```

time: 56.4 us -> 54.6 us (0.968)
  the two profiles are of different devices: /device:TPU:32 before, /device:TPU:16 now
where the time goes in v5:
time: 54.6 us; the launch traced here: 54.4 us
  blocking collectives  42.5 us (78%)
  waiting for transfers between devices  5.92 us (11%)
  Pallas kernels  4.5 us (8%)
  starting transfers between devices  0.78 us (1%)
  between operations  0.66 us (1%)
    all_to_all x2, blocking collectives, exchange(): lax.all_to_all(blocks, PEERS, split_axis=0, concat_axis=0, tiled=True)  42.5 us
    ppermute x1, waiting for transfers between devices, shards(): other = lax.ppermute(total.astype(BF16), 'yh', SWAP)  4.7 us
    pallas_call x4, Pallas kernels, local_call(): pl.pallas_call(kernel, out_shape=outs, in_specs=specs or [VMEM] * len(ope...  4.5 us
    ppermute x1, waiting for transfers between devices, shards(): total = total + lax.ppermute(total, 'c', SWAP)  1.22 us
  transfers between devices with their start and end apart: 2, of which 2 were waited for; matrix products, arithmetic and copies ran while one was open for 0% of the time, Pallas kernels for 0%

profile of v5, /device:TPU:16, one launch (start us, length us, event | category | flops | bytes accessed | tf_op | source)
XLA Modules:
  0.0 54.4 jit_solution(4216256037751799691)
XLA Ops:
  0.6 1.7 %shard_map.86 = (bf16[1024,128]{1,0:T(8,128)(2,1)S(1)}, f32[24,128]{1,0:T(8,128)S(1)}, bf16[128,256]{1,0:T(8,128)(2,1)S(1)}, bf16[4,256,256]{2,1,0:T(8,128)(2,1)S(1)}) custom-call(s32[16,256]{1,0:T(8,128)} %bitcast.23, s32[128,256]{1,0:T(8,128)} %bitcast.22, bf16[256,512]{1,0:T(8,128)(2,1)} %bitcast.17, bf16[512,512]{1,0:T(8,128)(2,1)} %constant.4.clone.forward_hbm, ...), custom_call_target="tpu_custom_call" | custom-call | flops 134217728 | bytes 1048576 | tf_op jit(solution)/shard_map/pallas_call | solution.py:271
  2.4 25.4 %all_to_all.10 = bf16[64,16,128]{2,1,0:T(8,128)(2,1)S(1)} all-to-all(bf16[64,16,128]{2,1,0:T(8,128)(2,1)S(1)} %bitcast.20), channel_id=1, replica_groups=mesh['yh'=2,'yl'=2,'zl'=4,'c'=2,'zh'=2,'x'=4] {'zl','yl','zh','x'}, dimensions={0} | all-to-all | bytes 524288 | tf_op jit(solution)/shard_map/all_to_all | solution.py:289
  27.8 0.6 %shard_map.87 = f32[4,24,128]{2,1,0:T(8,128)S(1)} custom-call(bf16[1024,128]{1,0:T(8,128)(2,1)S(1)} %bitcast.15, bf16[4,256,256]{2,1,0:T(8,128)(2,1)S(1)} %get-tuple-element.9.y_ref, bf16[128,256]{1,0:T(8,128)(2,1)S(1)} %get-tuple-element.10.x_ref, f32[24,128]{1,0:T(8,128)S(1)} %get-tuple-element.11.own_ref), custom_call_target="tpu_custom_call" | custom-call | flops 134217728 | bytes 1048576 | tf_op jit(solution)/shard_map/pallas_call | solution.py:271
  28.4 0.1 collective-permute-start
  28.5 1.2 %collective-permute-done = f32[4,24,128]{2,1,0:T(8,128)S(1)} collective-permute-done((f32[4,24,128]{2,1,0:T(8,128)S(1)}, f32[4,24,128]{2,1,0:T(8,128)S(1)}, u32[]{:S(2)}, u32[]{:S(2)}) %collective-permute-start) | collective-permute-done | bytes 49184 | tf_op jit(solution)/shard_map/ppermute | solution.py:339
  29.7 0.7 %collective-permute-start.1 = (bf16[4,24,128]{2,1,0:T(8,128)(2,1)S(1)}, bf16[4,24,128]{2,1,0:T(8,128)(2,1)S(1)}, u32[]{:S(2)}, u32[]{:S(2)}) collective-permute-start(bf16[4,24,128]{2,1,0:T(8,128)(2,1)S(1)} %get-tuple-element.14), channel_id=1, source_target_pairs={{0,128},{128,0},{1,129},{129,1},{2,130},{130,2},{3,131},{131,3},{4... | collective-permute-start | bytes 73736 | tf_op jit(solution)/shard_map/ppermute | solution.py:340
  30.4 4.7 %collective-permute-done.1.other_ref = bf16[4,24,128]{2,1,0:T(8,128)(2,1)S(1)} collective-permute-done((bf16[4,24,128]{2,1,0:T(8,128)(2,1)S(1)}, bf16[4,24,128]{2,1,0:T(8,128)(2,1)S(1)}, u32[]{:S(2)}, u32[]{:S(2)}) %collective-permute-start.1) | collective-permute-done | bytes 24608 | tf_op jit(solution)/shard_map/ppermute | solution.py:340
  35.1 0.0 copy-start.1
  35.1 1.1 %shard_map.88 = (f32[16,128]{1,0:T(8,128)}, bf16[1024,128]{1,0:T(8,128)(2,1)S(1)}) custom-call(f32[4,24,128]{2,1,0:T(8,128)S(1)} %get-tuple-element.15.sum_ref, bf16[4,24,128]{2,1,0:T(8,128)(2,1)S(1)} %collective-permute-done.1.other_ref, bf16[4,256,256]{2,1,0:T(8,128)(2,1)S(1)} %get-tuple-element.9.y_ref, bf16[128,256]{1,0:T(8,128)(2,1)S(1)} %get-tuple-element.10.x_ref), custom_call_target="tpu_custom_call" | custom-call | flops 134217728 | bytes 1048576 | tf_op jit(solution)/shard_map/pallas_call | solution.py:271
  36.3 0.0 copy-start
  36.3 17.1 %all_to_all.11 = bf16[64,16,128]{2,1,0:T(8,128)(2,1)S(1)} all-to-all(bf16[64,16,128]{2,1,0:T(8,128)(2,1)S(1)} %bitcast.19), channel_id=1, replica_groups=mesh['yh'=2,'yl'=2,'zl'=4,'c'=2,'zh'=2,'x'=4] {'zl','yl','zh','x'}, dimensions={0} | all-to-all | bytes 524288 | tf_op jit(solution)/shard_map/all_to_all | solution.py:289
  53.4 0.0 copy-done.1
  53.4 0.0 copy-done
  53.4 1.0 %shard_map.89 = bf16[256,512]{1,0:T(8,128)(2,1)} custom-call(bf16[1024,128]{1,0:T(8,128)(2,1)S(1)} %bitcast.16, bf16[256,512]{1,0:T(8,128)(2,1)S(1)} %bitcast.18, bf16[512,512]{1,0:T(8,128)(2,1)S(1)} %copy-done.1), custom_call_target="tpu_custom_call" | custom-call | flops 134217728 | bytes 1048576 | tf_op jit(solution)/shard_map/pallas_call | solution.py:271
  (1 shorter events, 0.0 us)
Async XLA Ops:
  28.4 1.3 %collective-permute-start = (f32[4,24,128]{2,1,0:T(8,128)S(1)}, f32[4,24,128]{2,1,0:T(8,128)S(1)}, u32[]{:S(2)}, u32[]{:S(2)}) collective-permute-start(f32[4,24,128]{2,1,0:T(8,128)S(1)} %shard_map.87), channel_id=1, source_target_pairs={{0,8},{8,0},{1,9},{9,1},{2,10},{10,2},{3,11},{11,3},{4,12},{12,4},... | collective-permute-start | bytes 147464 | tf_op jit(solution)/shard_map/ppermute | solution.py:339
  29.7 5.4 %collective-permute-start.1 = (bf16[4,24,128]{2,1,0:T(8,128)(2,1)S(1)}, bf16[4,24,128]{2,1,0:T(8,128)(2,1)S(1)}, u32[]{:S(2)}, u32[]{:S(2)}) collective-permute-start(bf16[4,24,128]{2,1,0:T(8,128)(2,1)S(1)} %get-tuple-element.14), channel_id=1, source_target_pairs={{0,128},{128,0},{1,129},{129,1},{2,130},{130,2},{3,131},{131,3},{4... | collective-permute-start | bytes 73736 | tf_op jit(solution)/shard_map/ppermute | solution.py:340
  35.1 18.3 %copy-start.1 = (bf16[512,512]{1,0:T(8,128)(2,1)S(1)}, bf16[512,512]{1,0:T(8,128)(2,1)}, u32[]{:S(2)}) copy-start(bf16[512,512]{1,0:T(8,128)(2,1)} %constant.5.clone.table_ref) | copy-start | bytes 1572868
  36.3 17.1 %copy-start = (bf16[8,32,512]{2,1,0:T(8,128)(2,1)S(1)}, bf16[8,32,512]{2,1,0:T(8,128)(2,1)}, u32[]{:S(2)}) copy-start(bf16[8,32,512]{2,1,0:T(8,128)(2,1)} %param.7) | copy-start | bytes 786436

commit v6 on v5

--- a/solution.py
+++ b/solution.py
@@ -18,7 +18,7 @@
 AXES = {"yh": 2, "yl": 2, "zl": 4, "c": 2, "zh": 2, "x": 4}
 SLAB = ("yh", "yl", "zl", "c")
 ROWS = ("zh", "x")
-PEERS = ("zl", "yl", "zh", "x")
+PEERS = ("zl", "zh", "x", "yl")
 TEAM = ("yh", "c")
 PLANES = 4
 SWAP = [(0, 1), (1, 0)]
@@ -124,9 +124,10 @@
     x_at = (lane >> 4 & 1) * 32 + (lane >> 1 & 3) * 8 + (lane >> 3 & 1) * 4 + (lane >> 5)
     x_at = x_at.astype(F32) * (1.0 / FINE)
     x_shift = (lane & 1).astype(F32) * 0.75
-    y_in = iota((32, LANES), 0).astype(F32)
-    block = iota((8, LANES), 0)
-    y_block = (block * 64 + at["yh"] * 512 + at["c"] * 32).astype(F32)
+    row = iota((8, LANES), 0)
+    y_in = row.astype(F32)
+    y_middle = (row * 8).astype(F32)
+    y_block = (row * 64 + at["yh"] * 512 + at["c"] * 32).astype(F32)
     plane = [plane_of({**at, "yh": p >> 1, "c": p & 1}) for p in range(PLANES)]
     for load in loads[:2]:
         load.wait()
@@ -136,9 +137,12 @@
     for p in range(PLANES):
         ky = (turned[pl.ds(plane[p], 1), :] + FINE / 2.0) * (1.0 / FINE)
         fine = phases(ky * y_in)
+        middle = phases(ky * y_middle)
         coarse = phases(ky * y_block)
+        inner = [product((middle[0][b : b + 1], middle[1][b : b + 1]), fine) for b in range(4)]
+        inner = [jnp.concatenate([m[i] for m in inner], axis=0) for i in range(2)]
         for b in range(8):
-            real, imag = product((coarse[0][b : b + 1], coarse[1][b : b + 1]), fine)
+            real, imag = product((coarse[0][b : b + 1], coarse[1][b : b + 1]), inner)
             y_table_ref[p, pl.ds(b * 32, 32), :LANES] = real.astype(BF16)
             y_table_ref[p, pl.ds(b * 32, 32), LANES:] = imag.astype(BF16)
         kx = jnp.sum(jnp.where(lane_plane == plane[p], x_own, 0.0), axis=1, keepdims=True)
@@ -169,9 +173,9 @@
     blocks = exchange_grains(blocks, 1, 32)
     left = [[[], []] for _ in range(PLANES)]
     for q in range(4):
-        rows = blocks[q].reshape(2, 2, 4, 16, LANES)
+        rows = blocks[q].reshape(2, 4, 2, 16, LANES)
         for i in range(2):
-            parts = exchange_grains([rows[i, :, x] for x in range(4)], 1, 2)
+            parts = exchange_grains([rows[:, x, i] for x in range(4)], 1, 2)
             for p in range(PLANES):
                 left[p][i].append(parts[p].reshape(-1, LANES))
     near, far = [], []
@@ -233,8 +237,8 @@
         for i in range(2):
             part = slice(i * LANES, i * LANES + LANES)
             parts = exchange_grains([planes[p][q, :, :, part] for p in range(PLANES)], 1, 2)
-            rows.append(jnp.stack(parts, axis=1).reshape(-1, LANES))
-        blocks.append(jnp.concatenate(rows, axis=0))
+            rows.append(jnp.stack(parts, axis=1))
+        blocks.append(jnp.stack(rows, axis=2).reshape(-1, LANES))
     blocks = exchange_grains(blocks, 1, 32)
     quarter = out_ref.shape[0] // 4
     for g in range(4):

time: 54.6 us -> 53.8 us (0.985)
  the two profiles are of different devices: /device:TPU:16 before, /device:TPU:32 now
where the time goes in v6:
time: 53.8 us; the launch traced here: 53.6 us
  blocking collectives  41.8 us (78%)
  Pallas kernels  4.47 us (8%)
  waiting for transfers between devices  3.65 us (7%)
  starting transfers between devices  3.04 us (6%)
  between operations  0.66 us (1%)
    all_to_all x2, blocking collectives, exchange(): lax.all_to_all(blocks, PEERS, split_axis=0, concat_axis=0, tiled=True)  41.8 us
    pallas_call x4, Pallas kernels, local_call(): pl.pallas_call(kernel, out_shape=outs, in_specs=specs or [VMEM] * len(ope...  4.47 us
    ppermute x1, starting transfers between devices, shards(): other = lax.ppermute(total.astype(BF16), 'yh', SWAP)  2.98 us
    ppermute x1, waiting for transfers between devices, shards(): other = lax.ppermute(total.astype(BF16), 'yh', SWAP)  2.44 us
    ppermute x1, waiting for transfers between devices, shards(): total = total + lax.ppermute(total, 'c', SWAP)  1.22 us
  transfers between devices with their start and end apart: 2, of which 2 were waited for; matrix products, arithmetic and copies ran while one was open for 0% of the time, Pallas kernels for 0%

profile of v6, /device:TPU:32, one launch (start us, length us, event | category | flops | bytes accessed | tf_op | source)
XLA Modules:
  0.0 53.6 jit_solution(17590469908070296751)
XLA Ops:
  0.6 1.7 %shard_map.86 = (bf16[1024,128]{1,0:T(8,128)(2,1)S(1)}, f32[24,128]{1,0:T(8,128)S(1)}, bf16[128,256]{1,0:T(8,128)(2,1)S(1)}, bf16[4,256,256]{2,1,0:T(8,128)(2,1)S(1)}) custom-call(s32[16,256]{1,0:T(8,128)} %bitcast.23, s32[128,256]{1,0:T(8,128)} %bitcast.22, bf16[256,512]{1,0:T(8,128)(2,1)} %bitcast.17, bf16[512,512]{1,0:T(8,128)(2,1)} %constant.4.clone.forward_hbm, ...), custom_call_target="tpu_custom_call" | custom-call | flops 134217728 | bytes 1048576 | tf_op jit(solution)/shard_map/pallas_call | solution.py:275
  2.3 24.7 %all_to_all.10 = bf16[64,16,128]{2,1,0:T(8,128)(2,1)S(1)} all-to-all(bf16[64,16,128]{2,1,0:T(8,128)(2,1)S(1)} %bitcast.20), channel_id=1, replica_groups=mesh['yh'=2,'yl'=2,'zl'=4,'c'=2,'zh'=2,'x'=4] {'zl','zh','x','yl'}, dimensions={0} | all-to-all | bytes 524288 | tf_op jit(solution)/shard_map/all_to_all | solution.py:293
  27.1 0.6 %shard_map.87 = f32[4,24,128]{2,1,0:T(8,128)S(1)} custom-call(bf16[1024,128]{1,0:T(8,128)(2,1)S(1)} %bitcast.15, bf16[4,256,256]{2,1,0:T(8,128)(2,1)S(1)} %get-tuple-element.9.y_ref, bf16[128,256]{1,0:T(8,128)(2,1)S(1)} %get-tuple-element.10.x_ref, f32[24,128]{1,0:T(8,128)S(1)} %get-tuple-element.11.own_ref), custom_call_target="tpu_custom_call" | custom-call | flops 134217728 | bytes 1048576 | tf_op jit(solution)/shard_map/pallas_call | solution.py:275
  27.7 0.1 collective-permute-start
  27.8 1.2 %collective-permute-done = f32[4,24,128]{2,1,0:T(8,128)S(1)} collective-permute-done((f32[4,24,128]{2,1,0:T(8,128)S(1)}, f32[4,24,128]{2,1,0:T(8,128)S(1)}, u32[]{:S(2)}, u32[]{:S(2)}) %collective-permute-start) | collective-permute-done | bytes 49184 | tf_op jit(solution)/shard_map/ppermute | solution.py:343
  29.0 3.0 %collective-permute-start.1 = (bf16[4,24,128]{2,1,0:T(8,128)(2,1)S(1)}, bf16[4,24,128]{2,1,0:T(8,128)(2,1)S(1)}, u32[]{:S(2)}, u32[]{:S(2)}) collective-permute-start(bf16[4,24,128]{2,1,0:T(8,128)(2,1)S(1)} %get-tuple-element.14), channel_id=1, source_target_pairs={{0,128},{128,0},{1,129},{129,1},{2,130},{130,2},{3,131},{131,3},{4... | collective-permute-start | bytes 73736 | tf_op jit(solution)/shard_map/ppermute | solution.py:344
  32.0 2.4 %collective-permute-done.1.other_ref = bf16[4,24,128]{2,1,0:T(8,128)(2,1)S(1)} collective-permute-done((bf16[4,24,128]{2,1,0:T(8,128)(2,1)S(1)}, bf16[4,24,128]{2,1,0:T(8,128)(2,1)S(1)}, u32[]{:S(2)}, u32[]{:S(2)}) %collective-permute-start.1) | collective-permute-done | bytes 24608 | tf_op jit(solution)/shard_map/ppermute | solution.py:344
  34.4 0.0 copy-start.1
  34.4 1.1 %shard_map.88 = (f32[16,128]{1,0:T(8,128)}, bf16[1024,128]{1,0:T(8,128)(2,1)S(1)}) custom-call(f32[4,24,128]{2,1,0:T(8,128)S(1)} %get-tuple-element.15.sum_ref, bf16[4,24,128]{2,1,0:T(8,128)(2,1)S(1)} %collective-permute-done.1.other_ref, bf16[4,256,256]{2,1,0:T(8,128)(2,1)S(1)} %get-tuple-element.9.y_ref, bf16[128,256]{1,0:T(8,128)(2,1)S(1)} %get-tuple-element.10.x_ref), custom_call_target="tpu_custom_call" | custom-call | flops 134217728 | bytes 1048576 | tf_op jit(solution)/shard_map/pallas_call | solution.py:275
  35.6 0.0 copy-start
  35.6 17.0 %all_to_all.11 = bf16[64,16,128]{2,1,0:T(8,128)(2,1)S(1)} all-to-all(bf16[64,16,128]{2,1,0:T(8,128)(2,1)S(1)} %bitcast.19), channel_id=1, replica_groups=mesh['yh'=2,'yl'=2,'zl'=4,'c'=2,'zh'=2,'x'=4] {'zl','zh','x','yl'}, dimensions={0} | all-to-all | bytes 524288 | tf_op jit(solution)/shard_map/all_to_all | solution.py:293
  52.6 0.0 copy-done.1
  52.6 0.0 copy-done
  52.6 1.0 %shard_map.89 = bf16[256,512]{1,0:T(8,128)(2,1)} custom-call(bf16[1024,128]{1,0:T(8,128)(2,1)S(1)} %bitcast.16, bf16[256,512]{1,0:T(8,128)(2,1)S(1)} %bitcast.18, bf16[512,512]{1,0:T(8,128)(2,1)S(1)} %copy-done.1), custom_call_target="tpu_custom_call" | custom-call | flops 134217728 | bytes 1048576 | tf_op jit(solution)/shard_map/pallas_call | solution.py:275
  (1 shorter events, 0.0 us)
Async XLA Ops:
  27.7 1.3 %collective-permute-start = (f32[4,24,128]{2,1,0:T(8,128)S(1)}, f32[4,24,128]{2,1,0:T(8,128)S(1)}, u32[]{:S(2)}, u32[]{:S(2)}) collective-permute-start(f32[4,24,128]{2,1,0:T(8,128)S(1)} %shard_map.87), channel_id=1, source_target_pairs={{0,8},{8,0},{1,9},{9,1},{2,10},{10,2},{3,11},{11,3},{4,12},{12,4},... | collective-permute-start | bytes 147464 | tf_op jit(solution)/shard_map/ppermute | solution.py:343
  29.0 5.4 %collective-permute-start.1 = (bf16[4,24,128]{2,1,0:T(8,128)(2,1)S(1)}, bf16[4,24,128]{2,1,0:T(8,128)(2,1)S(1)}, u32[]{:S(2)}, u32[]{:S(2)}) collective-permute-start(bf16[4,24,128]{2,1,0:T(8,128)(2,1)S(1)} %get-tuple-element.14), channel_id=1, source_target_pairs={{0,128},{128,0},{1,129},{129,1},{2,130},{130,2},{3,131},{131,3},{4... | collective-permute-start | bytes 73736 | tf_op jit(solution)/shard_map/ppermute | solution.py:344
  34.4 18.2 %copy-start.1 = (bf16[512,512]{1,0:T(8,128)(2,1)S(1)}, bf16[512,512]{1,0:T(8,128)(2,1)}, u32[]{:S(2)}) copy-start(bf16[512,512]{1,0:T(8,128)(2,1)} %constant.5.clone.table_ref) | copy-start | bytes 1572868
  35.6 17.0 %copy-start = (bf16[8,32,512]{2,1,0:T(8,128)(2,1)S(1)}, bf16[8,32,512]{2,1,0:T(8,128)(2,1)}, u32[]{:S(2)}) copy-start(bf16[8,32,512]{2,1,0:T(8,128)(2,1)} %param.7) | copy-start | bytes 786436
